TPU v7x, 256 devices: a whole 4x4x8 slice. The times are simulated.
256 devices in a mesh: sy: 16 (over x, y_hi, core), sx: 16 (over y_lo, z).
Axes of the slice: x: 4, y: 4 (y_hi: 2, y_lo: 2; y = y_hi * 2 + y_lo), z: 8, core: 2. Of those that a mesh axis runs over, the one named last changes fastest.
Arguments:
- object_tile: float32 [2, 2048, 2048], P(None, 'sy', 'sx'), may hold values from -5 to 5
- probe_modes: float32 [2, 2, 128, 128], replicated, may hold values from -4 to 4
- scan_offsets: int32 [16, 16, 4, 2], P('sy', 'sx'), may hold values from 0 to 128
- intensities: float32 [16, 16, 4, 128, 128], P('sy', 'sx'), may hold values from 0 to 2
Outputs:
- object_out: float32 [2, 2048, 2048], P(None, 'sy', 'sx')
- probe_out: float32 [2, 2, 128, 128], replicated
Inputs may be any that keep to these rules, and one draw needn't show every extreme that they name: `scan_offsets`: offsets are counted from 64 pixels above and to the left of the device's tile, so a patch stays within 64 pixels of its tile.
All inputs are finite; a program needn't handle non-finite values.
Results may differ from a plain program's by a relative error of at most 0.0003.
Values sent between devices are 32-bit elements; how exact they have to be, the bound alone decides.
A program may use at most 64 MiB of HBM per device.

v0:
```python
import jax
import jax.numpy as jnp
from jax import lax
from jax.sharding import PartitionSpec as P

ITERS = 2


HIGHEST = lax.Precision.HIGHEST
OBJECT_STEP = 0.5
PROBE_STEP = 2.0
REGULAR = 1.0


def extended(block, sides, width):
    for axis, dim in sides:
        count = lax.axis_size(axis)
        forward = [(i, i + 1) for i in range(count - 1)]
        backward = [(target, source) for source, target in forward]
        low = lax.ppermute(
            lax.slice_in_dim(block, block.shape[dim] - width, None, axis=dim), axis, forward
        )
        high = lax.ppermute(lax.slice_in_dim(block, 0, width, axis=dim), axis, backward)
        block = jnp.concatenate([low, block, high], axis=dim)
    return block


def shifted(value, axis, steps):
    count = lax.axis_size(axis)
    first, last = (max(0, -steps), min(count, count - steps))
    return lax.ppermute(value, axis, [(source, source + steps) for source in range(first, last)])


def tables(extent):
    index_line = jnp.arange(extent, dtype=jnp.int32)
    phase = index_line[:, None] * index_line[None, :] % extent
    angle = phase.astype(jnp.float32) * (2.0 * jnp.pi / extent)
    scale = 1.0 / jnp.sqrt(jnp.float32(extent))
    return (jnp.cos(angle) * scale, jnp.sin(angle) * scale)


def apply_left(matrix, values):
    return jnp.einsum("ux,bxy->buy", matrix, values, precision=HIGHEST)


def apply_right(values, matrix):
    return jnp.einsum("bxy,yv->bxv", values, matrix, precision=HIGHEST)


def transform(real_part, imag_part, cosine_table, sine_table, direction):
    half_real = apply_left(cosine_table, real_part) + direction * apply_left(sine_table, imag_part)
    half_imag = apply_left(cosine_table, imag_part) - direction * apply_left(sine_table, real_part)
    out_real = apply_right(half_real, cosine_table) + direction * apply_right(half_imag, sine_table)
    out_imag = apply_right(half_imag, cosine_table) - direction * apply_right(half_real, sine_table)
    return (out_real, out_imag)


def local_terms(canvas, probe_modes, offsets, measured):
    extent = probe_modes.shape[-1]
    mode_count = probe_modes.shape[0]
    positions = offsets.shape[0]
    patches = jax.vmap(
        lambda corner: lax.dynamic_slice(
            canvas, (jnp.int32(0), corner[0], corner[1]), (2, extent, extent)
        )
    )(offsets)
    object_real = patches[:, 0][:, None]
    object_imag = patches[:, 1][:, None]
    probe_real = probe_modes[:, 0][None]
    probe_imag = probe_modes[:, 1][None]
    exit_real = (probe_real * object_real - probe_imag * object_imag).reshape(
        positions * mode_count, extent, extent
    )
    exit_imag = (probe_real * object_imag + probe_imag * object_real).reshape(
        positions * mode_count, extent, extent
    )
    cosine_table, sine_table = tables(extent)
    spectrum_real, spectrum_imag = transform(exit_real, exit_imag, cosine_table, sine_table, 1.0)
    spectrum_real = spectrum_real.reshape(positions, mode_count, extent, extent)
    spectrum_imag = spectrum_imag.reshape(positions, mode_count, extent, extent)
    misfit = (
        jnp.sum(spectrum_real * spectrum_real + spectrum_imag * spectrum_imag, axis=1) - measured
    )
    back_real, back_imag = transform(
        (misfit[:, None] * spectrum_real).reshape(-1, extent, extent),
        (misfit[:, None] * spectrum_imag).reshape(-1, extent, extent),
        cosine_table,
        sine_table,
        -1.0,
    )
    back_real = back_real.reshape(positions, mode_count, extent, extent)
    back_imag = back_imag.reshape(positions, mode_count, extent, extent)
    grad_real = jnp.sum(probe_real * back_real + probe_imag * back_imag, axis=1)
    grad_imag = jnp.sum(probe_real * back_imag - probe_imag * back_real, axis=1)
    lighting = jnp.broadcast_to(
        jnp.sum(probe_real * probe_real + probe_imag * probe_imag, axis=1), grad_real.shape
    )
    terms = jnp.stack([grad_real, grad_imag, lighting], axis=1)
    numer_real = jnp.sum(object_real * back_real + object_imag * back_imag, axis=0)
    numer_imag = jnp.sum(object_real * back_imag - object_imag * back_real, axis=0)
    numerator = jnp.stack([numer_real, numer_imag], axis=1)
    denominator = jnp.sum(
        object_real[:, 0] * object_real[:, 0] + object_imag[:, 0] * object_imag[:, 0], axis=0
    )

    def place_patch(number, running):
        corner = offsets[number]
        existing = lax.dynamic_slice(
            running, (jnp.int32(0), corner[0], corner[1]), (3, extent, extent)
        )
        return lax.dynamic_update_slice(
            running, existing + terms[number], (jnp.int32(0), corner[0], corner[1])
        )

    gradients = lax.fori_loop(
        0, positions, place_patch, jnp.zeros((3,) + canvas.shape[1:], jnp.float32)
    )
    return (gradients, numerator, denominator)


def probe_update(probe_modes, numerator, denominator):
    extent = probe_modes.shape[-1]
    flat_numer = numerator.reshape(-1, extent * extent)
    flat_denom = denominator.reshape(extent * extent)
    flat_probe = probe_modes.reshape(-1, extent * extent)
    total_numer, total_denom = lax.psum((flat_numer, flat_denom), ("sy", "sx"))
    updated = flat_probe - PROBE_STEP * total_numer / (total_denom[None] + REGULAR)
    return updated.reshape(probe_modes.shape)


def fetch(current, halo_width):
    return extended(current, (("sy", 1), ("sx", 2)), halo_width)


def owner_sum(gradients, tile_size, halo_width):
    upper_rim = gradients[:, :halo_width]
    lower_rim = gradients[:, halo_width + tile_size :]
    from_above = shifted(lower_rim, "sy", 1)
    from_below = shifted(upper_rim, "sy", -1)
    middle = gradients[:, halo_width : halo_width + tile_size]
    middle = (
        middle.at[:, :halo_width].add(from_above).at[:, tile_size - halo_width :].add(from_below)
    )
    left_rim = middle[:, :, :halo_width]
    right_rim = middle[:, :, halo_width + tile_size :]
    from_left = shifted(right_rim, "sx", 1)
    from_right = shifted(left_rim, "sx", -1)
    owned = middle[:, :, halo_width : halo_width + tile_size]
    return (
        owned.at[:, :, :halo_width]
        .add(from_left)
        .at[:, :, tile_size - halo_width :]
        .add(from_right)
    )


def per_device(object_tile, probe_modes, scan_offsets, intensities):
    tile_size = object_tile.shape[1]
    halo_width = probe_modes.shape[-1] // 2
    offsets = scan_offsets[0, 0]
    measured = intensities[0, 0]
    current = object_tile
    for iteration in range(ITERS):
        canvas = fetch(current, halo_width)
        gradients, numerator, denominator = local_terms(canvas, probe_modes, offsets, measured)
        owned = owner_sum(gradients, tile_size, halo_width)
        fresh_probe = probe_update(probe_modes, numerator, denominator)
        current = current - OBJECT_STEP * owned[:2] / (owned[2:3] + REGULAR)
        probe_modes = fresh_probe
    return (current, probe_modes)


def solution(mesh):
    placed = (P(None, "sy", "sx"), P(), P("sy", "sx", None, None), P("sy", "sx", None, None, None))
    return jax.shard_map(
        per_device,
        mesh=mesh,
        in_specs=placed,
        out_specs=(P(None, "sy", "sx"), P()),
        check_vma=False,
    )
```

profile of v0, /device:TPU:1, one launch (start us, length us, event | category | flops | bytes accessed | tf_op | source)
XLA Modules:
  0.0 709.2 jit_solution(12127745365018270601)
XLA Ops:
  8.1 6.3 collective-permute-start
  14.5 1.9 collective-permute-start.1
  16.6 5.0 collective-permute-done.1
  21.7 3.6 collective-permute-start.2
  25.3 1.3 collective-permute-start.3
  26.6 1.9 collective-permute-done.2
  28.6 4.0 collective-permute-done.3
  32.9 8.2 %while.38 = (s32[]{:T(128)}, f32[2,256,256]{2,1,0:T(8,128)S(1)}, s32[4,3]{1,0:T(4,128)S(1)}, f32[4,2,128,128]{3,2,1,0:T(8,128)S(1)}, s32[]{:T(128)}) while((s32[]{:T(128)}, f32[2,256,256]{2,1,0:T(8,128)S(1)}, s32[4,3]{1,0:T(4,128)S(1)}, f32[4,2,128,128]{3,2,1,0:T(8,128)S(1)}, s32[]{:T(128)}) %tuple.147), condition=%wide.while_cond.8, body=%wide.while_body.8.sunk | while | flops 2 | bytes 262261 | solution.py:63
  33.6 1.4 bitcast_dynamic-update-slice_fusion.4
  35.6 1.4 bitcast_dynamic-update-slice_fusion.4
  37.7 1.4 bitcast_dynamic-update-slice_fusion.4
  39.7 1.4 bitcast_dynamic-update-slice_fusion.4
  59.4 2.0 add_reduce_fusion.3
  61.5 29.9 %while.36 = (s32[]{:T(128)}, f32[3,256,256]{2,1,0:T(8,128)S(1)}, s32[4,2]{0,1:T(2,128)S(1)}, f32[4,3,128,128]{3,2,1,0:T(8,128)S(1)}, s32[]{:T(128)}, /*index=5*/s32[]{:T(128)}, s32[]{:T(128)}) while((s32[]{:T(128)}, f32[3,256,256]{2,1,0:T(8,128)S(1)}, s32[4,2]{0,1:T(2,128)S(1)}, f32[4,3,128,128]{3,2,1,0:T(8,128)S(1)}, s32[]{:T(128)}, ...), condition=%wide.region_5.6_spmd, body=%wide.region_4.5_spmd.sunk | while | flops 49160 | bytes 983237 | solution.py:115
  66.1 3.0 dynamic_update_slice.16
  73.6 3.0 dynamic_update_slice.16
  81.2 2.9 dynamic_update_slice.16
  88.7 2.7 dynamic_update_slice.16
  92.2 4.5 collective-permute-start.4
  96.7 1.9 collective-permute-start.5
  101.4 3.9 collective-permute-done.5
  106.4 3.6 collective-permute-start.6
  110.0 240.5 %all-reduce.7.cloned.1.call-done = (f32[4,16384]{1,0:T(4,128)}, f32[16384]{0:T(1024)}) async-done(((f32[4,16384]{1,0:T(4,128)}, f32[16384]{0:T(1024)}), (f32[4,16384]{1,0:T(4,128)}, f32[16384]{0:T(1024)})) %all-reduce.7.cloned.1.call-update) | async-done | bytes 327696 | tf_op jit(solution)/shard_map/psum | solution.py:126
  351.4 1.3 collective-permute-start.7
  353.3 6.0 collective-permute-done.7
  361.5 5.8 collective-permute-start.8
  367.4 1.9 collective-permute-start.9
  369.6 4.9 collective-permute-done.9
  374.6 1.9 collective-permute-start.10
  376.5 1.3 collective-permute-start.11
  377.8 1.9 collective-permute-done.10
  379.8 3.8 collective-permute-done.11
  383.9 8.3 %while.39 = (s32[]{:T(128)}, f32[2,256,256]{2,1,0:T(8,128)S(1)}, s32[4,3]{1,0:T(4,128)S(1)}, f32[4,2,128,128]{3,2,1,0:T(8,128)S(1)}, s32[]{:T(128)}) while((s32[]{:T(128)}, f32[2,256,256]{2,1,0:T(8,128)S(1)}, s32[4,3]{1,0:T(4,128)S(1)}, f32[4,2,128,128]{3,2,1,0:T(8,128)S(1)}, s32[]{:T(128)}) %tuple.167), condition=%wide.while_cond.9, body=%wide.while_body.9.sunk | while | flops 2 | bytes 262261 | solution.py:63
  384.5 1.4 bitcast_dynamic-update-slice_fusion.5
  386.6 1.4 bitcast_dynamic-update-slice_fusion.5
  388.6 1.4 bitcast_dynamic-update-slice_fusion.5
  390.6 1.4 bitcast_dynamic-update-slice_fusion.5
  403.4 1.3 fusion.52
  412.8 29.9 %while.37 = (s32[]{:T(128)}, f32[3,256,256]{2,1,0:T(8,128)S(1)}, s32[4,2]{0,1:T(2,128)S(1)}, f32[4,3,128,128]{3,2,1,0:T(8,128)S(1)}, s32[]{:T(128)}, /*index=5*/s32[]{:T(128)}, s32[]{:T(128)}) while((s32[]{:T(128)}, f32[3,256,256]{2,1,0:T(8,128)S(1)}, s32[4,2]{0,1:T(2,128)S(1)}, f32[4,3,128,128]{3,2,1,0:T(8,128)S(1)}, s32[]{:T(128)}, ...), condition=%wide.region_16.17_spmd, body=%wide.region_15.16_spmd.sunk | while | flops 49160 | bytes 983237 | solution.py:115
  417.4 3.0 dynamic_update_slice.17
  425.0 3.0 dynamic_update_slice.17
  432.6 2.9 dynamic_update_slice.17
  440.1 2.7 dynamic_update_slice.17
  442.9 4.2 collective-permute-start.12
  447.1 1.9 collective-permute-start.13
  449.1 239.6 %all-reduce.5.cloned.1.call-done = (f32[4,16384]{1,0:T(4,128)}, f32[16384]{0:T(1024)}) async-done(((f32[4,16384]{1,0:T(4,128)}, f32[16384]{0:T(1024)}), (f32[4,16384]{1,0:T(4,128)}, f32[16384]{0:T(1024)})) %all-reduce.5.cloned.1.call-update) | async-done | bytes 327696 | tf_op jit(solution)/shard_map/psum | solution.py:126
  689.7 2.2 collective-permute-start.14
  696.0 4.2 collective-permute-done.15
  (179 shorter events, 65.8 us)
Async XLA Ops:
  7.2 343.3 %all-reduce.7.cloned.1.call-start = ((), (), s32[]{:S(2)}) async-start(), calls=%async_computation.1 | async-start | bytes 655360 | tf_op jit(solution)/shard_map/psum | solution.py:126
  7.2 9.2 %copy-start.11 = (s32[1,1,4,2]{2,3,1,0:T(2,128)S(1)}, s32[1,1,4,2]{2,3,1,0:T(2,128)}, u32[]{:S(2)}) copy-start(s32[1,1,4,2]{2,3,1,0:T(2,128)} %param.26) | copy-start | bytes 100
  8.1 8.5 %copy-start.3 = (f32[2,128,128]{2,1,0:T(8,128)S(1)}, f32[2,128,128]{2,1,0:T(8,128)}, u32[]{:S(2)}) copy-start(f32[2,128,128]{2,1,0:T(8,128)} %param.24) | copy-start | bytes 393220
  8.1 8.4 %collective-permute-start = (f32[2,64,128]{2,1,0:T(8,128)S(1)}, f32[2,64,128]{2,1,0:T(8,128)S(1)}, u32[]{:S(2)}, u32[]{:S(2)}) collective-permute-start(f32[2,64,128]{2,1,0:T(8,128)S(1)} %get-tuple-element.362), channel_id=1, source_target_pairs={{0,16},{16,32},{32,48},{48,64},{64,80},{80,96},{96,112},{112,128},... | collective-permute-start | bytes 196616 | tf_op jit(solution)/shard_map/ppermute | solution.py:20
  14.5 7.1 collective-permute-start.1
  21.6 5.0 copy-start.7
  21.7 6.8 collective-permute-start.2
  25.3 7.3 %collective-permute-start.3 = (f32[2,256,64]{2,1,0:T(8,128)S(1)}, f32[2,256,64]{2,1,0:T(8,128)S(1)}, u32[]{:S(2)}, u32[]{:S(2)}) collective-permute-start(f32[2,256,64]{2,1,0:T(8,128)S(1)} %get-tuple-element.355), channel_id=1, source_target_pairs={{1,0},{2,1},{3,2},{4,3},{5,4},{6,5},{7,6},{8,7},{9,8},{10,9},{11,1... | collective-permute-start | bytes 393224 | tf_op jit(solution)/shard_map/ppermute | solution.py:23
  41.2 0.7 copy-start
  49.8 1.2 copy-start.5
  92.1 6.5 copy-start.1
  92.1 6.5 copy-start.2
  92.2 8.3 %collective-permute-start.4 = (f32[3,64,256]{2,1,0:T(8,128)}, f32[3,64,256]{2,1,0:T(8,128)}, u32[]{:S(2)}, u32[]{:S(2)}) collective-permute-start(f32[3,64,256]{2,1,0:T(8,128)} %get-tuple-element.339), channel_id=1, source_target_pairs={{0,16},{16,32},{32,48},{48,64},{64,80},{80,96},{96,112},{112,128},... | collective-permute-start | bytes 589832 | tf_op jit(solution)/shard_map/ppermute | solution.py:31
  96.7 8.6 %collective-permute-start.5 = (f32[3,64,256]{2,1,0:T(8,128)S(1)}, f32[3,64,256]{2,1,0:T(8,128)}, u32[]{:S(2)}, u32[]{:S(2)}) collective-permute-start(f32[3,64,256]{2,1,0:T(8,128)S(1)} %get-tuple-element.338), channel_id=1, source_target_pairs={{16,0},{32,16},{48,32},{64,48},{80,64},{96,80},{112,96},{128,112},... | collective-permute-start | bytes 589832 | tf_op jit(solution)/shard_map/ppermute | solution.py:31
  100.4 588.2 %all-reduce.5.cloned.1.call-start = ((), (), s32[]{:S(2)}) async-start(), calls=%async_computation | async-start | bytes 655360 | tf_op jit(solution)/shard_map/psum | solution.py:126
  106.4 246.3 %collective-permute-start.6 = (f32[3,128,64]{2,1,0:T(8,128)S(1)}, f32[3,128,64]{2,1,0:T(8,128)S(1)}, u32[]{:S(2)}, u32[]{:S(2)}) collective-permute-start(f32[3,128,64]{2,1,0:T(8,128)S(1)} %get-tuple-element.345), channel_id=1, source_target_pairs={{0,1},{1,2},{2,3},{3,4},{4,5},{5,6},{6,7},{7,8},{8,9},{9,10},{10,1... | collective-permute-start | bytes 294920 | tf_op jit(solution)/shard_map/ppermute | solution.py:31
  351.4 8.0 %collective-permute-start.7 = (f32[3,128,64]{2,1,0:T(8,128)S(1)}, f32[3,128,64]{2,1,0:T(8,128)S(1)}, u32[]{:S(2)}, u32[]{:S(2)}) collective-permute-start(f32[3,128,64]{2,1,0:T(8,128)S(1)} %get-tuple-element.344), channel_id=1, source_target_pairs={{1,0},{2,1},{3,2},{4,3},{5,4},{6,5},{7,6},{8,7},{9,8},{10,9},{11,1... | collective-permute-start | bytes 294920 | tf_op jit(solution)/shard_map/ppermute | solution.py:31
  360.5 0.9 copy-start.4
  361.5 7.8 %copy-start.8 = (f32[2,2,128,128]{3,2,1,0:T(8,128)S(1)}, f32[2,2,128,128]{3,2,1,0:T(8,128)}, u32[]{:S(2)}) copy-start(f32[2,2,128,128]{3,2,1,0:T(8,128)} %param.25) | copy-start | bytes 786436
  361.5 7.8 %copy-start.9 = (f32[4,16384]{1,0:T(4,128)S(1)}, f32[4,16384]{1,0:T(4,128)}, u32[]{:S(2)}) copy-start(f32[4,16384]{1,0:T(4,128)} %get-tuple-element.324) | copy-start | bytes 786436
  361.5 8.1 %collective-permute-start.8 = (f32[2,64,128]{2,1,0:T(8,128)S(1)}, f32[2,64,128]{2,1,0:T(8,128)S(1)}, u32[]{:S(2)}, u32[]{:S(2)}) collective-permute-start(f32[2,64,128]{2,1,0:T(8,128)S(1)} %get-tuple-element.359), channel_id=1, source_target_pairs={{0,16},{16,32},{32,48},{48,64},{64,80},{80,96},{96,112},{112,128},... | collective-permute-start | bytes 196616 | tf_op jit(solution)/shard_map/ppermute | solution.py:20
  367.4 7.1 collective-permute-start.9
  374.6 5.2 collective-permute-start.10
  376.5 7.1 %collective-permute-start.11 = (f32[2,256,64]{2,1,0:T(8,128)S(1)}, f32[2,256,64]{2,1,0:T(8,128)S(1)}, u32[]{:S(2)}, u32[]{:S(2)}) collective-permute-start(f32[2,256,64]{2,1,0:T(8,128)S(1)} %get-tuple-element.349), channel_id=1, source_target_pairs={{1,0},{2,1},{3,2},{4,3},{5,4},{6,5},{7,6},{8,7},{9,8},{10,9},{11,1... | collective-permute-start | bytes 393224 | tf_op jit(solution)/shard_map/ppermute | solution.py:23
  401.0 1.2 copy-start.6
  442.9 246.6 %collective-permute-start.12 = (f32[3,64,256]{2,1,0:T(8,128)S(1)}, f32[3,64,256]{2,1,0:T(8,128)S(1)}, u32[]{:S(2)}, u32[]{:S(2)}) collective-permute-start(f32[3,64,256]{2,1,0:T(8,128)S(1)} %get-tuple-element.335), channel_id=1, source_target_pairs={{0,16},{16,32},{32,48},{48,64},{64,80},{80,96},{96,112},{112,128},... | collective-permute-start | bytes 589832 | tf_op jit(solution)/shard_map/ppermute | solution.py:31
  447.1 242.4 %collective-permute-start.13 = (f32[3,64,256]{2,1,0:T(8,128)S(1)}, f32[3,64,256]{2,1,0:T(8,128)S(1)}, u32[]{:S(2)}, u32[]{:S(2)}) collective-permute-start(f32[3,64,256]{2,1,0:T(8,128)S(1)} %get-tuple-element.334), channel_id=1, source_target_pairs={{16,0},{32,16},{48,32},{64,48},{80,64},{96,80},{112,96},{128,112},... | collective-permute-start | bytes 589832 | tf_op jit(solution)/shard_map/ppermute | solution.py:31
  689.6 2.4 copy-start.10
  689.7 5.6 collective-permute-start.14
  692.9 7.2 %collective-permute-start.15 = (f32[3,128,64]{2,1,0:T(8,128)S(1)}, f32[3,128,64]{2,1,0:T(8,128)S(1)}, u32[]{:S(2)}, u32[]{:S(2)}) collective-permute-start(f32[3,128,64]{2,1,0:T(8,128)S(1)} %get-tuple-element.342), channel_id=1, source_target_pairs={{1,0},{2,1},{3,2},{4,3},{5,4},{6,5},{7,6},{8,7},{9,8},{10,9},{11,1... | collective-permute-start | bytes 294920 | tf_op jit(solution)/shard_map/ppermute | solution.py:31
Sparse Core Ops, SparseCore 0:
  100.5 249.8 all-reduce.6
  443.0 245.6 all-reduce.4
where the time goes:
time: 721 us; the launch traced here: 709 us
  waiting for transfers between devices  517 us (72%)
  local copies, waits for them, and re-layouts  54.4 us (8%)
  starting transfers between devices  45.1 us (6%)
  matrix products  37.1 us (5%)
  loops' own time  30.8 us (4%)
  between operations  15.7 us (2%)
  other arithmetic  9.27 us (1%)
    psum x2, waiting for transfers between devices, probe_update(): total_numer, total_denom = lax.psum((flat_numer, flat_denom), ('sy', 'sx'))  480 us
    another operation x2, loops' own time, local_terms(): lax.fori_loop(0, positions, place_patch, jnp.zeros((3,) + canvas.shape[1:...  30.4 us
    dynamic_update_slice x8, local copies, waits for them, and re-layouts, place_patch(): lax.dynamic_update_slice(running, existing + terms[number], (jnp.int32(0)...  23.2 us
    ppermute x8, starting transfers between devices, shifted(): lax.ppermute(value, axis, [(source, source + steps) for source in range(f...  21 us
    dot_general x16, matrix products, apply_right(): return jnp.einsum('bxy,yv->bxv', values, matrix, precision=HIGHEST)  19 us
    dot_general x16, matrix products, apply_left(): return jnp.einsum('ux,bxy->buy', matrix, values, precision=HIGHEST)  18.1 us
    ppermute x4, waiting for transfers between devices, extended(): lax.ppermute(lax.slice_in_dim(block, 0, width, axis=dim), axis, backward)  17.7 us
    ppermute x4, starting transfers between devices, extended(): lax.ppermute(lax.slice_in_dim(block, block.shape[dim] - width, None, axis...  17.6 us
  transfers between devices with their start and end apart: 18, of which 12 were waited for; matrix products, arithmetic and copies ran while one was open for 1% of the time, Pallas kernels for 0%

commit v1 on v0

v1 whole, which is shorter than its diff:
```python
import functools

import numpy as np
import jax
import jax.numpy as jnp
from jax import lax
from jax.experimental import pallas as pl
from jax.experimental.pallas import tpu as pltpu
from jax.sharding import PartitionSpec as P

ITERS = 2
OBJECT_STEP = 0.5
PROBE_STEP = 2.0
REGULAR = 1.0
N = 128
HALF = 64
Y_LO = 2
MESH = pl.DeviceIdType.MESH
F32 = jnp.float32
BF16 = jnp.bfloat16

SIDES = [(-1, 0), (1, 0), (0, -1), (0, 1), (-1, -1), (1, -1), (-1, 1), (1, 1)]


def dft_tables():
    index = np.arange(N)
    angle = (index[:, None] * index[None, :] % N) * (2.0 * np.pi / N)
    scale = 1.0 / np.sqrt(float(N))
    cosine, sine = np.cos(angle) * scale, np.sin(angle) * scale
    forward = np.block([[cosine, -sine], [sine, cosine]])
    parts = []
    for matrix in (forward, forward.T):
        high = matrix.astype(np.float32).astype(BF16)
        low = (matrix - high.astype(np.float64)).astype(np.float32).astype(BF16)
        parts += [high, low]
    return np.stack(parts)


def split(value):
    high = value.astype(BF16)
    low = (value - high.astype(F32)).astype(BF16)
    return high, low


def dot(left, right):
    return jnp.dot(left, right, preferred_element_type=F32)


def swap_blocks(value):
    top = jnp.concatenate([value[:N, :N], value[N:, :N]], axis=1)
    bottom = jnp.concatenate([value[:N, N:], value[N:, N:]], axis=1)
    return jnp.concatenate([top, bottom], axis=0)


def kernel(n_sy, n_sx, positions, modes, offs, tile_in, probe_in, inten, tables,
           obj_out, prb_out,
           tile1, can_t, can_h, pack_l, pack_r, strip_l, strip_r,
           obj, back_g, nacc, pads, g_t, g_h, gp_l, gp_r, g_up, g_dn, f_l, f_r,
           l_t, l_h, l_up, l_dn, lf_l, lf_r, l_sum,
           n_buf, n_rcv, n_part, nz_rcv, m_buf, m_rcv, m_part, mz_rcv, p_buf,
           side_send, side_recv, all_send, all_recv):
    sy = lax.axis_index("sy")
    sx = lax.axis_index("sx")
    depth = n_sx // Y_LO
    group = n_sy * Y_LO
    blocks = group // modes
    rows = N // blocks
    y_lo = lax.div(sx, depth)
    z = lax.rem(sx, depth)
    me = sy * Y_LO + y_lo
    my_mode = lax.div(me, blocks)
    my_block = lax.rem(me, blocks)

    def side_dev(step):
        dy, dx = step
        return (lax.rem(sy + (n_sy + dy), n_sy), lax.rem(sx + (n_sx + dx), n_sx))

    def group_dev(other):
        return (lax.div(other, Y_LO), lax.rem(other, Y_LO) * depth + z)

    def z_dev(other):
        return (sy, y_lo * depth + other)

    lane = lax.broadcasted_iota(jnp.int32, (HALF, N), 1)
    lane_n = lax.broadcasted_iota(jnp.int32, (N, N), 1)
    has_u = jnp.where(sy > 0, 1, 0)
    has_d = jnp.where(sy < n_sy - 1, 1, 0)
    has_l = jnp.where(sx > 0, 1, 0)
    has_r = jnp.where(sx < n_sx - 1, 1, 0)

    def remote(src, dst, send, recv, dev):
        return pltpu.make_async_remote_copy(
            src_ref=src, dst_ref=dst, send_sem=send, recv_sem=recv,
            device_id=dev, device_id_type=MESH)

    def await_bytes(ref, sem):
        pltpu.make_async_copy(ref, ref, sem).wait()

    def fetch_copies(it, tile):
        top, bottom, both = pl.ds(0, HALF), pl.ds(HALF, HALF), pl.ds(0, N)
        c_top, c_mid, c_low = pl.ds(0, HALF), pl.ds(HALF, N), pl.ds(N + HALF, HALF)
        plan = [
            (tile.at[:, top, :], can_t.at[it, :, c_low, :]),
            (tile.at[:, bottom, :], can_t.at[it, :, c_top, :]),
            (pack_l.at[it, both], strip_r.at[it, c_mid]),
            (pack_r.at[it, both], strip_l.at[it, c_mid]),
            (pack_l.at[it, top], strip_r.at[it, c_low]),
            (pack_l.at[it, bottom], strip_r.at[it, c_top]),
            (pack_r.at[it, top], strip_l.at[it, c_low]),
            (pack_r.at[it, bottom], strip_l.at[it, c_top]),
        ]
        return [remote(src, dst, side_send.at[0, it, i], side_recv.at[0, it, i], side_dev(SIDES[i]))
                for i, (src, dst) in enumerate(plan)]

    def strip_copies(kind, it, src_t, src_l, src_r, up, down, left, right):
        top, mid, low = pl.ds(0, HALF), pl.ds(HALF, N), pl.ds(N + HALF, HALF)
        if kind == 1:
            vertical = [(src_t.at[:, top, :], up), (src_t.at[:, low, :], down)]
        else:
            vertical = [(src_t.at[top], up), (src_t.at[low], down)]
        plan = vertical + [
            (src_l.at[mid], right.at[mid]),
            (src_r.at[mid], left.at[mid]),
            (src_l.at[top], right.at[top]),
            (src_l.at[low], right.at[low]),
            (src_r.at[top], left.at[top]),
            (src_r.at[low], left.at[low]),
        ]
        return [remote(src, dst, side_send.at[kind, it, i], side_recv.at[kind, it, i],
                       side_dev(SIDES[i])) for i, (src, dst) in enumerate(plan)]

    def grad_copies(it):
        return strip_copies(1, it, g_t.at[it], gp_l.at[it], gp_r.at[it],
                            g_up.at[it], g_dn.at[it], f_l.at[it], f_r.at[it])

    def light_copies(it):
        return strip_copies(2, it, l_t.at[it], l_h.at[it], l_h.at[it],
                            l_up.at[it], l_dn.at[it], lf_l.at[it], lf_r.at[it])

    def pack(it, tile):
        real, rolled = tile[0], pltpu.roll(tile[1], HALF, 1)
        pack_l[it] = jnp.where(lane_n < HALF, real, rolled)
        pack_r[it] = jnp.where(lane_n >= HALF, real, rolled)

    def column_mask(column):
        return (lane_n >= column - HALF) & (lane_n < column + HALF)

    def assemble(it, tile):
        keep_re = (lane >= HALF * (1 - has_r)) & (lane < HALF + HALF * has_l)
        keep_im = (lane >= HALF * (1 - has_l)) & (lane < HALF + HALF * has_r)
        keep_u = lane < N * has_u
        keep_d = lane < N * has_d
        for c in range(2):
            can_t[it, c, pl.ds(HALF, N), :] = tile[c]
            top = can_t[it, c, pl.ds(0, HALF), :]
            can_t[it, c, pl.ds(0, HALF), :] = jnp.where(keep_u, top, 0.0)
            low = can_t[it, c, pl.ds(N + HALF, HALF), :]
            can_t[it, c, pl.ds(N + HALF, HALF), :] = jnp.where(keep_d, low, 0.0)
        for part in range(4):
            at = pl.ds(part * HALF, HALF)
            left, right = strip_l[it, at], strip_r[it, at]
            real = jnp.where(keep_re, jnp.where(lane < HALF, right, left), 0.0)
            imag = jnp.where(keep_im, jnp.where(lane < HALF, left, right), 0.0)
            if part == 0:
                real, imag = jnp.where(keep_u, real, 0.0), jnp.where(keep_u, imag, 0.0)
            if part == 3:
                real, imag = jnp.where(keep_d, real, 0.0), jnp.where(keep_d, imag, 0.0)
            can_h[it, 0, at, :] = real
            can_h[it, 1, at, :] = pltpu.roll(imag, HALF, 1)

    def extract(it):
        total = None
        for j in range(positions):
            row, column = offs[2 * j], offs[2 * j + 1]
            mask = column_mask(column)
            shift = lax.rem(HALF + N - column, N)
            for c in range(2):
                inner = can_t[it, c, pl.ds(row, N), :]
                outer = can_h[it, c, pl.ds(row, N), :]
                patch = pltpu.roll(jnp.where(mask, inner, outer), shift, 1)
                obj[j, c] = patch
                total = patch * patch if total is None else total + patch * patch
        m_buf[it] = total.reshape(blocks, rows, N)

    def place(channel, term):
        for j in range(positions):
            column = offs[2 * j + 1]
            mask = column_mask(column)
            turned = pltpu.roll(term(j), lax.rem(column + HALF, N), 1)
            pads[channel, 0, j, pl.ds(N, N), :] = jnp.where(mask, turned, 0.0)
            pads[channel, 1, j, pl.ds(N, N), :] = jnp.where(mask, 0.0, turned)

    def placed(channel, half):
        total = None
        for j in range(positions):
            window = pads[channel, half, j, pl.ds(N - offs[2 * j], 2 * N), :]
            total = window if total is None else total + window
        return total

    def probe_part(it, k, c):
        if it == 0:
            return probe_in[k, c]
        return p_buf[it - 1, k * blocks:(k + 1) * blocks, c].reshape(N, N)

    def light(it):
        bright = None
        for k in range(modes):
            for c in range(2):
                part = probe_part(it, k, c)
                bright = part * part if bright is None else bright + part * part
        place(2, lambda j: bright)
        l_t[it] = placed(2, 0)
        l_h[it] = placed(2, 1)

    def spread(what, it, source, target):
        def step(offset, carry):
            other = lax.rem(me + offset, group)
            remote(source(other), target(offset - 1), all_send.at[what, it], all_recv.at[what, it],
                   group_dev(other)).start()
            return carry
        lax.fori_loop(1, group, step, 0)

    def spread_z(what, it, source, target):
        def step(offset, carry):
            remote(source, target(offset - 1), all_send.at[what, it], all_recv.at[what, it],
                   z_dev(lax.rem(z + offset, depth))).start()
            return carry
        lax.fori_loop(1, depth, step, 0)

    def send_m(it):
        spread(0, it, lambda other: m_buf.at[it, lax.rem(other, blocks)], lambda s: m_rcv.at[it, s])

    def send_mz(it):
        await_bytes(m_rcv.at[it], all_recv.at[0, it])
        m_part[it] = m_buf[it, my_block] + jnp.sum(m_rcv[it], axis=0)
        spread_z(1, it, m_part.at[it], lambda s: mz_rcv.at[it, s])

    def send_n(it):
        spread(2, it, lambda other: n_buf.at[it, other], lambda s: n_rcv.at[it, s])

    def send_nz(it):
        await_bytes(n_rcv.at[it], all_recv.at[2, it])
        n_part[it] = n_buf[it, me] + jnp.sum(n_rcv[it], axis=0)
        spread_z(3, it, n_part.at[it], lambda s: nz_rcv.at[it, s])

    def send_p(it):
        await_bytes(mz_rcv.at[it], all_recv.at[1, it])
        denominator = m_part[it] + jnp.sum(mz_rcv[it], axis=0)
        await_bytes(nz_rcv.at[it], all_recv.at[3, it])
        numerator = n_part[it] + jnp.sum(nz_rcv[it], axis=0)
        for c in range(2):
            if it == 0:
                old = probe_in[my_mode, c, pl.ds(pl.multiple_of(my_block * rows, rows), rows), :]
            else:
                old = p_buf[it - 1, me, c]
            p_buf[it, me, c] = old - PROBE_STEP * numerator[c] / (denominator + REGULAR)
        spread(4, it, lambda other: p_buf.at[it, me], lambda s: p_buf.at[it, me])

    def wait_p(it):
        await_bytes(p_buf.at[it, pl.ds(0, group - 1)], all_recv.at[4, it])

    def waves(it):
        nacc[...] = jnp.zeros_like(nacc)

        def position(j, carry):
            o_re, o_im = obj[j, 0], obj[j, 1]
            wave = []
            for k in range(modes):
                p_re, p_im = probe_part(it, k, 0), probe_part(it, k, 1)
                wave.append(jnp.concatenate(
                    [p_re * o_re - p_im * o_im, p_re * o_im + p_im * o_re], axis=1))
            x_h, x_l = split(jnp.concatenate(wave, axis=0))
            half = dot(x_h, tables[0]) + dot(x_l, tables[0]) + dot(x_h, tables[1])
            b_h, b_l = split(swap_blocks(half))
            spec = dot(tables[2], b_h) + dot(tables[2], b_l) + dot(tables[3], b_h)
            power = spec[:N] * spec[:N] + spec[N:] * spec[N:]
            misfit = power[:, :N] + power[:, N:] - inten[j]
            wide = jnp.concatenate([misfit, misfit], axis=1)
            d_h, d_l = split(jnp.concatenate([spec[:N] * wide, spec[N:] * wide], axis=0))
            half = dot(tables[0], d_h) + dot(tables[0], d_l) + dot(tables[1], d_h)
            e_h, e_l = split(swap_blocks(half))
            chi = dot(e_h, tables[2]) + dot(e_l, tables[2]) + dot(e_h, tables[3])
            g_re, g_im = None, None
            for k in range(modes):
                c_re, c_im = chi[k * N:(k + 1) * N, :N], chi[k * N:(k + 1) * N, N:]
                nacc[k, 0] += o_re * c_re + o_im * c_im
                nacc[k, 1] += o_re * c_im - o_im * c_re
                p_re, p_im = probe_part(it, k, 0), probe_part(it, k, 1)
                a_re = p_re * c_re + p_im * c_im
                a_im = p_re * c_im - p_im * c_re
                g_re = a_re if g_re is None else g_re + a_re
                g_im = a_im if g_im is None else g_im + a_im
            back_g[j, 0] = g_re
            back_g[j, 1] = g_im
            return carry

        lax.fori_loop(0, positions, position, 0)
        for k in range(modes):
            for c in range(2):
                n_buf[it, k * blocks:(k + 1) * blocks, c] = nacc[k, c].reshape(blocks, rows, N)

    def gradient(it):
        for c in range(2):
            place(c, lambda j: back_g[j, c])
            g_t[it, c] = placed(c, 0)
            g_h[c] = placed(c, 1)
        wide = lax.broadcasted_iota(jnp.int32, (2 * N, N), 1)
        real, rolled = g_h[0], pltpu.roll(g_h[1], HALF, 1)
        gp_l[it] = jnp.where(wide >= HALF, real, rolled)
        gp_r[it] = jnp.where(wide < HALF, real, rolled)

    def strip_sum(strip):
        top, low = strip[pl.ds(0, HALF)], strip[pl.ds(N + HALF, HALF)]
        upper = strip[pl.ds(HALF, HALF)] + jnp.where(lane < N * has_u, low, 0.0)
        lower = strip[pl.ds(N, HALF)] + jnp.where(lane < N * has_d, top, 0.0)
        return jnp.concatenate([upper, lower], axis=0)

    def own_light(it):
        from_l, from_r = strip_sum(lf_l.at[it]), strip_sum(lf_r.at[it])
        from_up = jnp.where(lane < N * has_u, l_dn[it], 0.0)
        from_down = jnp.where(lane < N * has_d, l_up[it], 0.0)
        total = l_t[it, pl.ds(HALF, N), :] + jnp.concatenate([from_up, from_down], axis=0)
        total += jnp.where(lane_n < HALF * has_l, from_l, 0.0)
        total += jnp.where(lane_n >= N - HALF * has_r, from_r, 0.0)
        l_sum[it] = total

    def update(it, old, new):
        from_l, from_r = strip_sum(f_l.at[it]), strip_sum(f_r.at[it])
        weight = l_sum[it] + REGULAR
        for c in range(2):
            from_up = jnp.where(lane < N * has_u, g_dn[it, c], 0.0)
            from_down = jnp.where(lane < N * has_d, g_up[it, c], 0.0)
            total = g_t[it, c, pl.ds(HALF, N), :] + jnp.concatenate([from_up, from_down], axis=0)
            left = from_l if c == 0 else pltpu.roll(from_l, HALF, 1)
            right = from_r if c == 0 else pltpu.roll(from_r, HALF, 1)
            total += jnp.where(lane_n < HALF * has_l, left, 0.0)
            total += jnp.where(lane_n >= N - HALF * has_r, right, 0.0)
            new[c] = old[c] - OBJECT_STEP * total / weight

    barrier = pltpu.get_barrier_semaphore()
    for step in SIDES:
        pl.semaphore_signal(barrier, inc=1, device_id=side_dev(step), device_id_type=MESH)

    def greet(offset, carry):
        pl.semaphore_signal(barrier, inc=1, device_id=group_dev(lax.rem(me + offset, group)),
                            device_id_type=MESH)
        return carry

    def greet_z(offset, carry):
        pl.semaphore_signal(barrier, inc=1, device_id=z_dev(lax.rem(z + offset, depth)),
                            device_id_type=MESH)
        return carry

    lax.fori_loop(1, group, greet, 0)
    lax.fori_loop(1, depth, greet_z, 0)
    pack(0, tile_in)
    pl.semaphore_wait(barrier, len(SIDES) + group - 1 + depth - 1)

    for copy in fetch_copies(0, tile_in):
        copy.start()
    for channel in range(3):
        for half in range(2):
            for j in range(positions):
                pads[channel, half, j, pl.ds(0, N), :] = jnp.zeros((N, N), F32)
                pads[channel, half, j, pl.ds(2 * N, N), :] = jnp.zeros((N, N), F32)
    light(0)
    for copy in light_copies(0):
        copy.start()

    tiles = [tile_in, tile1, obj_out]
    for it in range(ITERS):
        for copy in fetch_copies(it, tiles[it]):
            copy.wait_recv()
        assemble(it, tiles[it])
        extract(it)
        send_m(it)
        if it > 0:
            wait_p(it - 1)
            light(it)
            for copy in light_copies(it):
                copy.start()
        waves(it)
        send_n(it)
        send_mz(it)
        gradient(it)
        for copy in grad_copies(it):
            copy.start()
        for copy in light_copies(it):
            copy.wait_recv()
        own_light(it)
        send_nz(it)
        for copy in grad_copies(it):
            copy.wait_recv()
        update(it, tiles[it], tiles[it + 1])
        if it + 1 < ITERS:
            pack(it + 1, tiles[it + 1])
            for copy in fetch_copies(it + 1, tiles[it + 1]):
                copy.start()
        send_p(it)
    wait_p(ITERS - 1)
    for k in range(modes):
        for c in range(2):
            prb_out[k, c] = probe_part(ITERS, k, c)

    for it in range(ITERS):
        for copies in (fetch_copies(it, tiles[it]), grad_copies(it), light_copies(it)):
            for copy in copies:
                copy.wait_send()
        await_bytes(m_rcv.at[it], all_send.at[0, it])
        await_bytes(mz_rcv.at[it], all_send.at[1, it])
        await_bytes(n_rcv.at[it], all_send.at[2, it])
        await_bytes(nz_rcv.at[it], all_send.at[3, it])
        await_bytes(p_buf.at[it, pl.ds(0, group - 1)], all_send.at[4, it])


def per_device(n_sy, n_sx, object_tile, probe_modes, scan_offsets, intensities):
    positions = scan_offsets.shape[2]
    modes = probe_modes.shape[0]
    depth = n_sx // Y_LO
    group = n_sy * Y_LO
    blocks = group // modes
    rows = N // blocks
    offsets = scan_offsets.reshape(positions * 2)
    measured = intensities[0, 0]
    tables = jnp.asarray(dft_tables())
    vmem = functools.partial(pltpu.VMEM, dtype=F32)
    it = ITERS
    scratch = [
        vmem((2, N, N)), vmem((it, 2, 2 * N, N)), vmem((it, 2, 2 * N, N)),
        vmem((it, N, N)), vmem((it, N, N)), vmem((it, 2 * N, N)), vmem((it, 2 * N, N)),
        vmem((positions, 2, N, N)), vmem((positions, 2, N, N)), vmem((modes, 2, N, N)),
        vmem((3, 2, positions, 3 * N, N)), vmem((it, 2, 2 * N, N)), vmem((2, 2 * N, N)),
        vmem((it, 2 * N, N)), vmem((it, 2 * N, N)), vmem((it, 2, HALF, N)), vmem((it, 2, HALF, N)),
        vmem((it, 2 * N, N)), vmem((it, 2 * N, N)),
        vmem((it, 2 * N, N)), vmem((it, 2 * N, N)), vmem((it, HALF, N)), vmem((it, HALF, N)),
        vmem((it, 2 * N, N)), vmem((it, 2 * N, N)), vmem((it, N, N)),
        vmem((it, group, 2, rows, N)), vmem((it, group - 1, 2, rows, N)), vmem((it, 2, rows, N)),
        vmem((it, depth - 1, 2, rows, N)),
        vmem((it, blocks, rows, N)), vmem((it, group - 1, rows, N)), vmem((it, rows, N)),
        vmem((it, depth - 1, rows, N)), vmem((it, group, 2, rows, N)),
        pltpu.SemaphoreType.DMA((3, it, len(SIDES))), pltpu.SemaphoreType.DMA((3, it, len(SIDES))),
        pltpu.SemaphoreType.DMA((5, it)), pltpu.SemaphoreType.DMA((5, it)),
    ]
    in_vmem = pl.BlockSpec(memory_space=pltpu.VMEM)
    return pl.pallas_call(
        functools.partial(kernel, n_sy, n_sx, positions, modes),
        out_shape=(jax.ShapeDtypeStruct(object_tile.shape, F32),
                   jax.ShapeDtypeStruct(probe_modes.shape, F32)),
        in_specs=[pl.BlockSpec(memory_space=pltpu.SMEM)] + [in_vmem] * 4,
        out_specs=(in_vmem, in_vmem),
        scratch_shapes=scratch,
        compiler_params=pltpu.CompilerParams(collective_id=0, has_side_effects=True),
    )(offsets, object_tile, probe_modes, measured, tables)


def solution(mesh):
    placed = (P(None, "sy", "sx"), P(), P("sy", "sx", None, None), P("sy", "sx", None, None, None))
    return jax.shard_map(
        functools.partial(per_device, mesh.shape["sy"], mesh.shape["sx"]),
        mesh=mesh,
        in_specs=placed,
        out_specs=(P(None, "sy", "sx"), P()),
        check_vma=False,
    )
```

time: 721 us -> 76.8 us (0.11); the launches traced: 709 us -> 76.6 us
  waiting for transfers between devices: 517 us -> 0 us
  Pallas kernels: 0 us -> 72.3 us
  local copies, waits for them, and re-layouts: 54.4 us -> 3.68 us
  starting transfers between devices: 45.1 us -> 0 us
  matrix products: 37.1 us -> 0 us
  loops' own time: 30.8 us -> 0 us
  between operations: 15.7 us -> 0.66 us
  other arithmetic: 9.27 us -> 0 us
    psum x2 -> x0, waiting for transfers between devices: 480 us -> none  [probe_update(): total_numer, total_denom = lax.psum((flat_numer, flat_denom), ('sy', 'sx'))]
    pallas_call x0 -> x1, Pallas kernels: none -> 72.3 us  [per_device(): pl.pallas_call(functools.partial(kernel, n_sy, n_sx, positions, modes), o...]
    ppermute x16 -> x0, starting transfers between devices: 45.1 us -> none  [the longest x8 21 us: shifted(): lax.ppermute(value, axis, [(source, source + steps) for source in range(f...]
    dot_general x32 -> x0, matrix products: 37.1 us -> none  [the longest x16 19 us: apply_right(): return jnp.einsum('bxy,yv->bxv', values, matrix, precision=HIGHEST)]
    ppermute x16 -> x0, waiting for transfers between devices: 36.8 us -> none  [the longest x4 17.7 us: extended(): lax.ppermute(lax.slice_in_dim(block, 0, width, axis=dim), axis, backward)]
    another operation x4 -> x0, loops' own time: 30.8 us -> none  [the longest x2 30.4 us: local_terms(): lax.fori_loop(0, positions, place_patch, jnp.zeros((3,) + canvas.shape[1:...]
    dynamic_update_slice x8 -> x0, local copies, waits for them, and re-layouts: 23.2 us -> none  [place_patch(): lax.dynamic_update_slice(running, existing + terms[number], (jnp.int32(0)...]
    gather x24 -> x0, local copies, waits for them, and re-layouts: 16.1 us -> none
  transfers between devices with their start and end apart: 18 -> 0, of which waited for: 12 -> 0; matrix products, arithmetic and copies ran while one was open for 1% -> 0% of each run, Pallas kernels for 0% -> 0%
where the time goes in v1:
time: 76.8 us; the launch traced here: 76.6 us
  Pallas kernels  72.3 us (94%)
  local copies, waits for them, and re-layouts  3.68 us (5%)
    pallas_call x1, Pallas kernels, per_device(): pl.pallas_call(functools.partial(kernel, n_sy, n_sx, positions, modes), o...  72.3 us
    unnamed x7, local copies, waits for them, and re-layouts  3.08 us

profile of v1, /device:TPU:1, one launch (start us, length us, event | category | flops | bytes accessed | tf_op | source)
XLA Modules:
  0.0 76.6 jit_solution(16041140487389697734)
XLA Ops:
  0.6 0.0 copy-start.1
  0.6 0.7 copy-done.1
  1.3 0.1 copy.8
  1.4 0.6 reshape.7.offs
  2.0 72.3 %shard_map.68 = (f32[2,128,128]{2,1,0:T(8,128)}, f32[2,2,128,128]{3,2,1,0:T(8,128)}) custom-call(s32[8]{0:T(128)} %reshape.7.offs, f32[2,128,128]{2,1,0:T(8,128)} %tile_in.1, f32[2,2,128,128]{3,2,1,0:T(8,128)} %probe_in.1, f32[4,128,128]{2,1,0:T(8,128)} %bitcast.1, bf16[4,256,256]{2,1,0:T(8,128)(2,1)} %constant.2.clone.tables), custom_call_target="tpu_custom_call" | custom-call | tf_op jit(solution)/shard_map/pallas_call | solution.py:445
  74.3 0.0 copy-start
  74.3 1.6 %copy.11 = f32[2,128,128]{2,1,0:T(8,128)} copy(f32[2,128,128]{2,1,0:T(8,128)} %get-tuple-element.4) | data formatting | bytes 262144
  75.9 0.0 copy-done
  75.9 0.7 copy.12
Async XLA Ops:
  0.6 0.7 copy-start.1
  74.3 1.6 %copy-start = (f32[2,2,128,128]{3,2,1,0:T(8,128)S(1)}, f32[2,2,128,128]{3,2,1,0:T(8,128)}, u32[]{:S(2)}) copy-start(f32[2,2,128,128]{3,2,1,0:T(8,128)} %get-tuple-element.5) | copy-start | bytes 786436

commit v2 on v1

--- a/solution.py
+++ b/solution.py
@@ -19,7 +19,7 @@
 F32 = jnp.float32
 BF16 = jnp.bfloat16
 
-SIDES = [(-1, 0), (1, 0), (0, -1), (0, 1), (-1, -1), (1, -1), (-1, 1), (1, 1)]
+SIDES = [(-1, -1), (1, -1), (-1, 1), (1, 1), (-1, 0), (1, 0), (0, -1), (0, 1)]
 
 
 def dft_tables():
@@ -52,34 +52,49 @@
     return jnp.concatenate([top, bottom], axis=0)
 
 
-def kernel(n_sy, n_sx, positions, modes, offs, tile_in, probe_in, inten, tables,
+def far_first(count):
+    return sorted(range(count), key=lambda d: -min(d, count - d))
+
+
+def kernel(n_sy, n_sx, positions, modes, offs, tile_hbm, probe_hbm, inten_hbm, tables_hbm,
            obj_out, prb_out,
-           tile1, can_t, can_h, pack_l, pack_r, strip_l, strip_r,
+           tile_in, probe_in, inten, tables, tile1, can_t, can_h, pack_l, pack_r, strip_l, strip_r,
            obj, back_g, nacc, pads, g_t, g_h, gp_l, gp_r, g_up, g_dn, f_l, f_r,
-           l_t, l_h, l_up, l_dn, lf_l, lf_r, l_sum,
+           l_t, l_h, lp_l, lp_r, l_up, l_dn, lf_l, lf_r, l_sum,
            n_buf, n_rcv, n_part, nz_rcv, m_buf, m_rcv, m_part, mz_rcv, p_buf,
-           side_send, side_recv, all_send, all_recv):
+           side_send, side_recv, all_send, all_recv, load_sem):
     sy = lax.axis_index("sy")
     sx = lax.axis_index("sx")
     depth = n_sx // Y_LO
     group = n_sy * Y_LO
     blocks = group // modes
     rows = N // blocks
+    cores = 2
+    n_yh = min(2, n_sy // cores)
+    n_x, n_y = n_sy // (cores * n_yh), n_yh * Y_LO
+    core = lax.rem(sy, cores)
+    x = lax.div(sy, cores * n_yh)
     y_lo = lax.div(sx, depth)
+    y = lax.rem(lax.div(sy, cores), n_yh) * Y_LO + y_lo
     z = lax.rem(sx, depth)
     me = sy * Y_LO + y_lo
     my_mode = lax.div(me, blocks)
     my_block = lax.rem(me, blocks)
+    x_part = [lax.rem(x + d, n_x) * (cores * n_yh * Y_LO) for d in range(n_x)]
+    y_at = [lax.rem(y + d, n_y) for d in range(n_y)]
+    y_part = [lax.div(v, Y_LO) * (cores * Y_LO) + lax.rem(v, Y_LO) for v in y_at]
+    c_part = [lax.rem(core + d, cores) * Y_LO for d in range(cores)]
+    y_col = [lax.rem(v, Y_LO) * depth + z for v in y_at]
+    peers = [(dx, dy, dc) for dx in far_first(n_x) for dy in far_first(n_y) for dc in range(cores)
+             if dx or dy or dc]
+    peers.sort(key=lambda p: -(min(p[0], n_x - p[0]) + min(p[1], n_y - p[1])))
+    peer_index = [x_part[dx] + y_part[dy] + c_part[dc] for dx, dy, dc in peers]
+    peer_dev = [(lax.div(at, Y_LO), y_col[p[1]]) for at, p in zip(peer_index, peers)]
+    z_devs = [(sy, y_lo * depth + lax.rem(z + d, depth)) for d in far_first(depth) if d]
 
     def side_dev(step):
         dy, dx = step
         return (lax.rem(sy + (n_sy + dy), n_sy), lax.rem(sx + (n_sx + dx), n_sx))
-
-    def group_dev(other):
-        return (lax.div(other, Y_LO), lax.rem(other, Y_LO) * depth + z)
-
-    def z_dev(other):
-        return (sy, y_lo * depth + other)
 
     lane = lax.broadcasted_iota(jnp.int32, (HALF, N), 1)
     lane_n = lax.broadcasted_iota(jnp.int32, (N, N), 1)
@@ -100,42 +115,42 @@
         top, bottom, both = pl.ds(0, HALF), pl.ds(HALF, HALF), pl.ds(0, N)
         c_top, c_mid, c_low = pl.ds(0, HALF), pl.ds(HALF, N), pl.ds(N + HALF, HALF)
         plan = [
+            (pack_l.at[it, top], strip_r.at[it, c_low]),
+            (pack_l.at[it, bottom], strip_r.at[it, c_top]),
+            (pack_r.at[it, top], strip_l.at[it, c_low]),
+            (pack_r.at[it, bottom], strip_l.at[it, c_top]),
             (tile.at[:, top, :], can_t.at[it, :, c_low, :]),
             (tile.at[:, bottom, :], can_t.at[it, :, c_top, :]),
             (pack_l.at[it, both], strip_r.at[it, c_mid]),
             (pack_r.at[it, both], strip_l.at[it, c_mid]),
-            (pack_l.at[it, top], strip_r.at[it, c_low]),
-            (pack_l.at[it, bottom], strip_r.at[it, c_top]),
-            (pack_r.at[it, top], strip_l.at[it, c_low]),
-            (pack_r.at[it, bottom], strip_l.at[it, c_top]),
         ]
         return [remote(src, dst, side_send.at[0, it, i], side_recv.at[0, it, i], side_dev(SIDES[i]))
                 for i, (src, dst) in enumerate(plan)]
 
-    def strip_copies(kind, it, src_t, src_l, src_r, up, down, left, right):
-        top, mid, low = pl.ds(0, HALF), pl.ds(HALF, N), pl.ds(N + HALF, HALF)
-        if kind == 1:
-            vertical = [(src_t.at[:, top, :], up), (src_t.at[:, low, :], down)]
-        else:
-            vertical = [(src_t.at[top], up), (src_t.at[low], down)]
-        plan = vertical + [
-            (src_l.at[mid], right.at[mid]),
-            (src_r.at[mid], left.at[mid]),
+    def strip_copies(kind, it, unit, vertical, src_l, src_r, left, right):
+        top, mid, low = pl.ds(0, unit), pl.ds(unit, 2 * unit), pl.ds(3 * unit, unit)
+        plan = [
             (src_l.at[top], right.at[top]),
             (src_l.at[low], right.at[low]),
             (src_r.at[top], left.at[top]),
             (src_r.at[low], left.at[low]),
+        ] + vertical + [
+            (src_l.at[mid], right.at[mid]),
+            (src_r.at[mid], left.at[mid]),
         ]
         return [remote(src, dst, side_send.at[kind, it, i], side_recv.at[kind, it, i],
                        side_dev(SIDES[i])) for i, (src, dst) in enumerate(plan)]
 
     def grad_copies(it):
-        return strip_copies(1, it, g_t.at[it], gp_l.at[it], gp_r.at[it],
-                            g_up.at[it], g_dn.at[it], f_l.at[it], f_r.at[it])
+        vertical = [(g_t.at[it, :, pl.ds(0, HALF), :], g_up.at[it]),
+                    (g_t.at[it, :, pl.ds(N + HALF, HALF), :], g_dn.at[it])]
+        return strip_copies(1, it, HALF, vertical, gp_l.at[it], gp_r.at[it], f_l.at[it], f_r.at[it])
 
     def light_copies(it):
-        return strip_copies(2, it, l_t.at[it], l_h.at[it], l_h.at[it],
-                            l_up.at[it], l_dn.at[it], lf_l.at[it], lf_r.at[it])
+        vertical = [(l_t.at[it, pl.ds(0, HALF)], l_up.at[it]),
+                    (l_t.at[it, pl.ds(N + HALF, HALF)], l_dn.at[it])]
+        return strip_copies(2, it, HALF // 2, vertical, lp_l.at[it], lp_r.at[it],
+                            lf_l.at[it], lf_r.at[it])
 
     def pack(it, tile):
         real, rolled = tile[0], pltpu.roll(tile[1], HALF, 1)
@@ -171,7 +186,7 @@
     def extract(it):
         total = None
         for j in range(positions):
-            row, column = offs[2 * j], offs[2 * j + 1]
+            row, column = offs[0, 0, 0, j], offs[0, 0, 1, j]
             mask = column_mask(column)
             shift = lax.rem(HALF + N - column, N)
             for c in range(2):
@@ -184,7 +199,7 @@
 
     def place(channel, term):
         for j in range(positions):
-            column = offs[2 * j + 1]
+            column = offs[0, 0, 1, j]
             mask = column_mask(column)
             turned = pltpu.roll(term(j), lax.rem(column + HALF, N), 1)
             pads[channel, 0, j, pl.ds(N, N), :] = jnp.where(mask, turned, 0.0)
@@ -193,7 +208,7 @@
     def placed(channel, half):
         total = None
         for j in range(positions):
-            window = pads[channel, half, j, pl.ds(N - offs[2 * j], 2 * N), :]
+            window = pads[channel, half, j, pl.ds(N - offs[0, 0, 0, j], 2 * N), :]
             total = window if total is None else total + window
         return total
 
@@ -210,22 +225,24 @@
                 bright = part * part if bright is None else bright + part * part
         place(2, lambda j: bright)
         l_t[it] = placed(2, 0)
-        l_h[it] = placed(2, 1)
+        l_h[...] = placed(2, 1)
+        half = HALF // 2
+        low_lanes = lax.broadcasted_iota(jnp.int32, (half, N), 1) < HALF
+        for part in range(4):
+            first = l_h[pl.ds(part * HALF, half), :]
+            second = l_h[pl.ds(part * HALF + half, half), :]
+            at = pl.ds(part * half, half)
+            lp_l[it, at, :] = jnp.where(low_lanes, pltpu.roll(first, HALF, 1), second)
+            lp_r[it, at, :] = jnp.where(low_lanes, first, pltpu.roll(second, HALF, 1))
 
     def spread(what, it, source, target):
-        def step(offset, carry):
-            other = lax.rem(me + offset, group)
-            remote(source(other), target(offset - 1), all_send.at[what, it], all_recv.at[what, it],
-                   group_dev(other)).start()
-            return carry
-        lax.fori_loop(1, group, step, 0)
+        for slot, (other, dev) in enumerate(zip(peer_index, peer_dev)):
+            remote(source(other), target(slot), all_send.at[what, it], all_recv.at[what, it],
+                   dev).start()
 
     def spread_z(what, it, source, target):
-        def step(offset, carry):
-            remote(source, target(offset - 1), all_send.at[what, it], all_recv.at[what, it],
-                   z_dev(lax.rem(z + offset, depth))).start()
-            return carry
-        lax.fori_loop(1, depth, step, 0)
+        for slot, dev in enumerate(z_devs):
+            remote(source, target(slot), all_send.at[what, it], all_recv.at[what, it], dev).start()
 
     def send_m(it):
         spread(0, it, lambda other: m_buf.at[it, lax.rem(other, blocks)], lambda s: m_rcv.at[it, s])
@@ -316,7 +333,21 @@
         return jnp.concatenate([upper, lower], axis=0)
 
     def own_light(it):
-        from_l, from_r = strip_sum(lf_l.at[it]), strip_sum(lf_r.at[it])
+        half = HALF // 2
+
+        def unpacked(strip, here):
+            parts = []
+            for part in range(4):
+                block = strip[pl.ds(part * half, half), :]
+                turned = pltpu.roll(block, HALF, 1)
+                parts += [turned, block] if here else [block, turned]
+            low = jnp.where(lane < N * has_u, jnp.concatenate(parts[6:], axis=0), 0.0)
+            top = jnp.where(lane < N * has_d, jnp.concatenate(parts[:2], axis=0), 0.0)
+            upper = jnp.concatenate(parts[2:4], axis=0) + low
+            lower = jnp.concatenate(parts[4:6], axis=0) + top
+            return jnp.concatenate([upper, lower], axis=0)
+
+        from_r, from_l = unpacked(lf_r.at[it], True), unpacked(lf_l.at[it], False)
         from_up = jnp.where(lane < N * has_u, l_dn[it], 0.0)
         from_down = jnp.where(lane < N * has_d, l_up[it], 0.0)
         total = l_t[it, pl.ds(HALF, N), :] + jnp.concatenate([from_up, from_down], axis=0)
@@ -338,23 +369,16 @@
             new[c] = old[c] - OBJECT_STEP * total / weight
 
     barrier = pltpu.get_barrier_semaphore()
-    for step in SIDES:
-        pl.semaphore_signal(barrier, inc=1, device_id=side_dev(step), device_id_type=MESH)
-
-    def greet(offset, carry):
-        pl.semaphore_signal(barrier, inc=1, device_id=group_dev(lax.rem(me + offset, group)),
-                            device_id_type=MESH)
-        return carry
-
-    def greet_z(offset, carry):
-        pl.semaphore_signal(barrier, inc=1, device_id=z_dev(lax.rem(z + offset, depth)),
-                            device_id_type=MESH)
-        return carry
-
-    lax.fori_loop(1, group, greet, 0)
-    lax.fori_loop(1, depth, greet_z, 0)
+    greeted = [side_dev(step) for step in SIDES] + peer_dev + z_devs
+    for dev in greeted:
+        pl.semaphore_signal(barrier, inc=1, device_id=dev, device_id_type=MESH)
+    loads = [pltpu.make_async_copy(src, dst, load_sem.at[i]) for i, (src, dst) in enumerate(
+        [(tile_hbm, tile_in), (probe_hbm, probe_in), (tables_hbm, tables), (inten_hbm, inten)])]
+    for load in loads:
+        load.start()
+    loads[0].wait()
     pack(0, tile_in)
-    pl.semaphore_wait(barrier, len(SIDES) + group - 1 + depth - 1)
+    pl.semaphore_wait(barrier, len(greeted))
 
     for copy in fetch_copies(0, tile_in):
         copy.start()
@@ -363,10 +387,13 @@
             for j in range(positions):
                 pads[channel, half, j, pl.ds(0, N), :] = jnp.zeros((N, N), F32)
                 pads[channel, half, j, pl.ds(2 * N, N), :] = jnp.zeros((N, N), F32)
+    loads[1].wait()
     light(0)
     for copy in light_copies(0):
         copy.start()
 
+    loads[2].wait()
+    loads[3].wait()
     tiles = [tile_in, tile1, obj_out]
     for it in range(ITERS):
         for copy in fetch_copies(it, tiles[it]):
@@ -376,15 +403,16 @@
         send_m(it)
         if it > 0:
             wait_p(it - 1)
-            light(it)
-            for copy in light_copies(it):
-                copy.start()
         waves(it)
         send_n(it)
         send_mz(it)
         gradient(it)
         for copy in grad_copies(it):
             copy.start()
+        if it > 0:
+            light(it)
+            for copy in light_copies(it):
+                copy.start()
         for copy in light_copies(it):
             copy.wait_recv()
         own_light(it)
@@ -420,33 +448,37 @@
     group = n_sy * Y_LO
     blocks = group // modes
     rows = N // blocks
-    offsets = scan_offsets.reshape(positions * 2)
+    offsets = scan_offsets.transpose(0, 1, 3, 2)
     measured = intensities[0, 0]
     tables = jnp.asarray(dft_tables())
     vmem = functools.partial(pltpu.VMEM, dtype=F32)
     it = ITERS
     scratch = [
+        vmem(object_tile.shape), vmem(probe_modes.shape), vmem(measured.shape),
+        pltpu.VMEM(tables.shape, BF16),
         vmem((2, N, N)), vmem((it, 2, 2 * N, N)), vmem((it, 2, 2 * N, N)),
         vmem((it, N, N)), vmem((it, N, N)), vmem((it, 2 * N, N)), vmem((it, 2 * N, N)),
         vmem((positions, 2, N, N)), vmem((positions, 2, N, N)), vmem((modes, 2, N, N)),
         vmem((3, 2, positions, 3 * N, N)), vmem((it, 2, 2 * N, N)), vmem((2, 2 * N, N)),
         vmem((it, 2 * N, N)), vmem((it, 2 * N, N)), vmem((it, 2, HALF, N)), vmem((it, 2, HALF, N)),
         vmem((it, 2 * N, N)), vmem((it, 2 * N, N)),
-        vmem((it, 2 * N, N)), vmem((it, 2 * N, N)), vmem((it, HALF, N)), vmem((it, HALF, N)),
-        vmem((it, 2 * N, N)), vmem((it, 2 * N, N)), vmem((it, N, N)),
+        vmem((it, 2 * N, N)), vmem((2 * N, N)), vmem((it, N, N)), vmem((it, N, N)),
+        vmem((it, HALF, N)), vmem((it, HALF, N)),
+        vmem((it, N, N)), vmem((it, N, N)), vmem((it, N, N)),
         vmem((it, group, 2, rows, N)), vmem((it, group - 1, 2, rows, N)), vmem((it, 2, rows, N)),
         vmem((it, depth - 1, 2, rows, N)),
         vmem((it, blocks, rows, N)), vmem((it, group - 1, rows, N)), vmem((it, rows, N)),
         vmem((it, depth - 1, rows, N)), vmem((it, group, 2, rows, N)),
         pltpu.SemaphoreType.DMA((3, it, len(SIDES))), pltpu.SemaphoreType.DMA((3, it, len(SIDES))),
         pltpu.SemaphoreType.DMA((5, it)), pltpu.SemaphoreType.DMA((5, it)),
+        pltpu.SemaphoreType.DMA((4,)),
     ]
     in_vmem = pl.BlockSpec(memory_space=pltpu.VMEM)
     return pl.pallas_call(
         functools.partial(kernel, n_sy, n_sx, positions, modes),
         out_shape=(jax.ShapeDtypeStruct(object_tile.shape, F32),
                    jax.ShapeDtypeStruct(probe_modes.shape, F32)),
-        in_specs=[pl.BlockSpec(memory_space=pltpu.SMEM)] + [in_vmem] * 4,
+        in_specs=[pl.BlockSpec(memory_space=pltpu.SMEM)] + [pl.BlockSpec(memory_space=pl.ANY)] * 4,
         out_specs=(in_vmem, in_vmem),
         scratch_shapes=scratch,
         compiler_params=pltpu.CompilerParams(collective_id=0, has_side_effects=True),

time: 76.8 us -> 75.2 us (0.979)
  local copies, waits for them, and re-layouts: 3.68 us -> 2.32 us
    unnamed x7 -> x4, local copies, waits for them, and re-layouts: 3.08 us -> 2.32 us
where the time goes in v2:
time: 75.2 us; the launch traced here: 75.1 us
  Pallas kernels  72.1 us (96%)
  local copies, waits for them, and re-layouts  2.32 us (3%)
    pallas_call x1, Pallas kernels, per_device(): pl.pallas_call(functools.partial(kernel, n_sy, n_sx, positions, modes), o...  72.1 us
    unnamed x4, local copies, waits for them, and re-layouts  2.32 us

profile of v2, /device:TPU:1, one launch (start us, length us, event | category | flops | bytes accessed | tf_op | source)
XLA Modules:
  0.0 75.1 jit_solution(8696767801860171890)
XLA Ops:
  0.6 72.1 %shard_map.68 = (f32[2,128,128]{2,1,0:T(8,128)}, f32[2,2,128,128]{3,2,1,0:T(8,128)}) custom-call(s32[1,1,2,4]{3,2,1,0:T(2,128)} %bitcast.3, f32[2,128,128]{2,1,0:T(8,128)} %tile_hbm.1, f32[2,2,128,128]{3,2,1,0:T(8,128)} %probe_hbm.1, f32[4,128,128]{2,1,0:T(8,128)} %bitcast.2, bf16[4,256,256]{2,1,0:T(8,128)(2,1)} %constant.2.clone.tables_hbm), custom_call_target="tpu_custom_call" | custom-call | tf_op jit(solution)/shard_map/pallas_call | solution.py:477
  72.7 0.0 copy-start
  72.7 1.6 %copy.9 = f32[2,128,128]{2,1,0:T(8,128)} copy(f32[2,128,128]{2,1,0:T(8,128)} %get-tuple-element.4) | data formatting | bytes 262144
  74.4 0.0 copy-done
  74.4 0.7 copy.10
Async XLA Ops:
  72.7 1.6 %copy-start = (f32[2,2,128,128]{3,2,1,0:T(8,128)S(1)}, f32[2,2,128,128]{3,2,1,0:T(8,128)}, u32[]{:S(2)}) copy-start(f32[2,2,128,128]{3,2,1,0:T(8,128)} %get-tuple-element.5) | copy-start | bytes 786436

commit v3 on v2

--- a/solution.py
+++ b/solution.py
@@ -58,17 +58,15 @@
 
 def kernel(n_sy, n_sx, positions, modes, offs, tile_hbm, probe_hbm, inten_hbm, tables_hbm,
            obj_out, prb_out,
-           tile_in, probe_in, inten, tables, tile1, can_t, can_h, pack_l, pack_r, strip_l, strip_r,
-           obj, back_g, nacc, pads, g_t, g_h, gp_l, gp_r, g_up, g_dn, f_l, f_r,
-           l_t, l_h, lp_l, lp_r, l_up, l_dn, lf_l, lf_r, l_sum,
-           n_buf, n_rcv, n_part, nz_rcv, m_buf, m_rcv, m_part, mz_rcv, p_buf,
-           side_send, side_recv, all_send, all_recv, load_sem):
+           tile_in, probe_in, inten, tables, near_offs,
+           tile1, can_t, can_h, pack_l, pack_r, strip_l, strip_r,
+           obj, nacc, pads, bright_pad, g_t, g_h, gp_l, gp_r, g_up, g_dn, f_l, f_r, l_sum,
+           n_buf, n_pre, n_chip, n_rcv, n_part, nz_rcv,
+           m_buf, m_pre, m_chip, m_rcv, m_part, mz_rcv, p_buf,
+           side_send, side_recv, pair_send, pair_recv, all_send, all_recv, load_sem):
     sy = lax.axis_index("sy")
     sx = lax.axis_index("sx")
     depth = n_sx // Y_LO
-    group = n_sy * Y_LO
-    blocks = group // modes
-    rows = N // blocks
     cores = 2
     n_yh = min(2, n_sy // cores)
     n_x, n_y = n_sy // (cores * n_yh), n_yh * Y_LO
@@ -77,20 +75,19 @@
     y_lo = lax.div(sx, depth)
     y = lax.rem(lax.div(sy, cores), n_yh) * Y_LO + y_lo
     z = lax.rem(sx, depth)
-    me = sy * Y_LO + y_lo
-    my_mode = lax.div(me, blocks)
-    my_block = lax.rem(me, blocks)
-    x_part = [lax.rem(x + d, n_x) * (cores * n_yh * Y_LO) for d in range(n_x)]
+    x_at = [lax.rem(x + d, n_x) for d in range(n_x)]
     y_at = [lax.rem(y + d, n_y) for d in range(n_y)]
-    y_part = [lax.div(v, Y_LO) * (cores * Y_LO) + lax.rem(v, Y_LO) for v in y_at]
-    c_part = [lax.rem(core + d, cores) * Y_LO for d in range(cores)]
+    y_row = [lax.div(v, Y_LO) * cores + core for v in y_at]
     y_col = [lax.rem(v, Y_LO) * depth + z for v in y_at]
-    peers = [(dx, dy, dc) for dx in far_first(n_x) for dy in far_first(n_y) for dc in range(cores)
-             if dx or dy or dc]
+    blocks = n_x * n_y
+    rows = N // blocks
+    me = x * n_y + y
+    peers = [(dx, dy) for dx in far_first(n_x) for dy in far_first(n_y) if dx or dy]
     peers.sort(key=lambda p: -(min(p[0], n_x - p[0]) + min(p[1], n_y - p[1])))
-    peer_index = [x_part[dx] + y_part[dy] + c_part[dc] for dx, dy, dc in peers]
-    peer_dev = [(lax.div(at, Y_LO), y_col[p[1]]) for at, p in zip(peer_index, peers)]
+    peer_index = [x_at[dx] * n_y + y_at[dy] for dx, dy in peers]
+    peer_dev = [(x_at[dx] * (cores * n_yh) + y_row[dy], y_col[dy]) for dx, dy in peers]
     z_devs = [(sy, y_lo * depth + lax.rem(z + d, depth)) for d in far_first(depth) if d]
+    partner = (sy + 1 - 2 * core, sx)
 
     def side_dev(step):
         dy, dx = step
@@ -146,11 +143,9 @@
                     (g_t.at[it, :, pl.ds(N + HALF, HALF), :], g_dn.at[it])]
         return strip_copies(1, it, HALF, vertical, gp_l.at[it], gp_r.at[it], f_l.at[it], f_r.at[it])
 
-    def light_copies(it):
-        vertical = [(l_t.at[it, pl.ds(0, HALF)], l_up.at[it]),
-                    (l_t.at[it, pl.ds(N + HALF, HALF)], l_dn.at[it])]
-        return strip_copies(2, it, HALF // 2, vertical, lp_l.at[it], lp_r.at[it],
-                            lf_l.at[it], lf_r.at[it])
+    def offset_copies():
+        return [remote(offs, near_offs.at[i], side_send.at[2, 0, i], side_recv.at[2, 0, i],
+                       side_dev(step)) for i, step in enumerate(SIDES)]
 
     def pack(it, tile):
         real, rolled = tile[0], pltpu.roll(tile[1], HALF, 1)
@@ -196,14 +191,14 @@
                 obj[j, c] = patch
                 total = patch * patch if total is None else total + patch * patch
         m_buf[it] = total.reshape(blocks, rows, N)
-
-    def place(channel, term):
-        for j in range(positions):
-            column = offs[0, 0, 1, j]
-            mask = column_mask(column)
-            turned = pltpu.roll(term(j), lax.rem(column + HALF, N), 1)
-            pads[channel, 0, j, pl.ds(N, N), :] = jnp.where(mask, turned, 0.0)
-            pads[channel, 1, j, pl.ds(N, N), :] = jnp.where(mask, 0.0, turned)
+        pair(0, it, m_buf.at[it], m_pre.at[it]).start()
+
+    def place(channel, j, term):
+        column = offs[0, 0, 1, j]
+        mask = column_mask(column)
+        turned = pltpu.roll(term, lax.rem(column + HALF, N), 1)
+        pads[channel, 0, j, pl.ds(N, N), :] = jnp.where(mask, turned, 0.0)
+        pads[channel, 1, j, pl.ds(N, N), :] = jnp.where(mask, 0.0, turned)
 
     def placed(channel, half):
         total = None
@@ -215,7 +210,7 @@
     def probe_part(it, k, c):
         if it == 0:
             return probe_in[k, c]
-        return p_buf[it - 1, k * blocks:(k + 1) * blocks, c].reshape(N, N)
+        return p_buf[it - 1, c, :, k].reshape(N, N)
 
     def light(it):
         bright = None
@@ -223,17 +218,33 @@
             for c in range(2):
                 part = probe_part(it, k, c)
                 bright = part * part if bright is None else bright + part * part
-        place(2, lambda j: bright)
-        l_t[it] = placed(2, 0)
-        l_h[...] = placed(2, 1)
-        half = HALF // 2
-        low_lanes = lax.broadcasted_iota(jnp.int32, (half, N), 1) < HALF
-        for part in range(4):
-            first = l_h[pl.ds(part * HALF, half), :]
-            second = l_h[pl.ds(part * HALF + half, half), :]
-            at = pl.ds(part * half, half)
-            lp_l[it, at, :] = jnp.where(low_lanes, pltpu.roll(first, HALF, 1), second)
-            lp_r[it, at, :] = jnp.where(low_lanes, first, pltpu.roll(second, HALF, 1))
+        bright_pad[pl.ds(N + HALF, N), :] = bright
+        total = jnp.zeros((N, N), F32)
+        for dy in (-1, 0, 1):
+            for dx in (-1, 0, 1):
+                inside = jnp.where((sy + dy >= 0) & (sy + dy < n_sy)
+                                   & (sx + dx >= 0) & (sx + dx < n_sx), 0, 4 * N)
+                table = near_offs.at[SIDES.index((-dy, -dx))] if dx or dy else offs
+
+                def position(j, running, dy=dy, dx=dx, inside=inside, table=table):
+                    column = table[0, 0, 1, j]
+                    window = bright_pad[pl.ds(2 * N - N * dy - table[0, 0, 0, j], N), :]
+                    turned = pltpu.roll(window, lax.rem(column + HALF, N), 1)
+                    first = column + (N * dx - HALF) + inside
+                    mask = (lane_n >= first) & (lane_n < first + N)
+                    return running + jnp.where(mask, turned, 0.0)
+
+                total = lax.fori_loop(0, positions, position, total)
+        l_sum[it] = total
+
+    def pair(what, it, src, dst):
+        return remote(src, dst, pair_send.at[what, it], pair_recv.at[what, it], partner)
+
+    def n_pair(it):
+        return pair(1, it, n_buf.at[it, 1 - core], n_pre.at[it])
+
+    def p_pair(it):
+        return pair(2, it, p_buf.at[it, core], p_buf.at[it, core])
 
     def spread(what, it, source, target):
         for slot, (other, dev) in enumerate(zip(peer_index, peer_dev)):
@@ -245,41 +256,46 @@
             remote(source, target(slot), all_send.at[what, it], all_recv.at[what, it], dev).start()
 
     def send_m(it):
-        spread(0, it, lambda other: m_buf.at[it, lax.rem(other, blocks)], lambda s: m_rcv.at[it, s])
+        pair(0, it, m_buf.at[it], m_pre.at[it]).wait_recv()
+        m_chip[it] = m_buf[it] + m_pre[it]
+        spread(0, it, lambda other: m_chip.at[it, other], lambda s: m_rcv.at[it, s])
 
     def send_mz(it):
         await_bytes(m_rcv.at[it], all_recv.at[0, it])
-        m_part[it] = m_buf[it, my_block] + jnp.sum(m_rcv[it], axis=0)
+        m_part[it] = m_chip[it, me] + jnp.sum(m_rcv[it], axis=0)
         spread_z(1, it, m_part.at[it], lambda s: mz_rcv.at[it, s])
 
     def send_n(it):
-        spread(2, it, lambda other: n_buf.at[it, other], lambda s: n_rcv.at[it, s])
+        n_pair(it).wait_recv()
+        n_chip[it] = n_buf[it, core] + n_pre[it]
+        spread(2, it, lambda other: n_chip.at[it, other], lambda s: n_rcv.at[it, s])
 
     def send_nz(it):
         await_bytes(n_rcv.at[it], all_recv.at[2, it])
-        n_part[it] = n_buf[it, me] + jnp.sum(n_rcv[it], axis=0)
+        n_part[it] = n_chip[it, me] + jnp.sum(n_rcv[it], axis=0)
         spread_z(3, it, n_part.at[it], lambda s: nz_rcv.at[it, s])
 
     def send_p(it):
         await_bytes(mz_rcv.at[it], all_recv.at[1, it])
-        denominator = m_part[it] + jnp.sum(mz_rcv[it], axis=0)
+        weight = m_part[it] + jnp.sum(mz_rcv[it], axis=0) + REGULAR
         await_bytes(nz_rcv.at[it], all_recv.at[3, it])
         numerator = n_part[it] + jnp.sum(nz_rcv[it], axis=0)
-        for c in range(2):
+        for k in range(modes):
             if it == 0:
-                old = probe_in[my_mode, c, pl.ds(pl.multiple_of(my_block * rows, rows), rows), :]
+                old = probe_in[k, core, pl.ds(pl.multiple_of(me * rows, rows), rows), :]
             else:
-                old = p_buf[it - 1, me, c]
-            p_buf[it, me, c] = old - PROBE_STEP * numerator[c] / (denominator + REGULAR)
-        spread(4, it, lambda other: p_buf.at[it, me], lambda s: p_buf.at[it, me])
-
-    def wait_p(it):
-        await_bytes(p_buf.at[it, pl.ds(0, group - 1)], all_recv.at[4, it])
+                old = p_buf[it - 1, core, me, k]
+            p_buf[it, core, me, k] = old - PROBE_STEP * numerator[k] / weight
+        spread(4, it, lambda other: p_buf.at[it, core, me], lambda s: p_buf.at[it, core, me])
+
+    def forward_p(it):
+        await_bytes(p_buf.at[it, 0, pl.ds(0, blocks - 1)], all_recv.at[4, it])
+        p_pair(it).start()
 
     def waves(it):
         nacc[...] = jnp.zeros_like(nacc)
 
-        def position(j, carry):
+        def position(j):
             o_re, o_im = obj[j, 0], obj[j, 1]
             wave = []
             for k in range(modes):
@@ -307,18 +323,20 @@
                 a_im = p_re * c_im - p_im * c_re
                 g_re = a_re if g_re is None else g_re + a_re
                 g_im = a_im if g_im is None else g_im + a_im
-            back_g[j, 0] = g_re
-            back_g[j, 1] = g_im
-            return carry
-
-        lax.fori_loop(0, positions, position, 0)
+            place(0, j, g_re)
+            place(1, j, g_im)
+
+        for j in range(positions):
+            position(j)
+            if j == 0:
+                send_m(it)
         for k in range(modes):
             for c in range(2):
-                n_buf[it, k * blocks:(k + 1) * blocks, c] = nacc[k, c].reshape(blocks, rows, N)
+                n_buf[it, c, :, k] = nacc[k, c].reshape(blocks, rows, N)
+        n_pair(it).start()
 
     def gradient(it):
         for c in range(2):
-            place(c, lambda j: back_g[j, c])
             g_t[it, c] = placed(c, 0)
             g_h[c] = placed(c, 1)
         wide = lax.broadcasted_iota(jnp.int32, (2 * N, N), 1)
@@ -331,29 +349,6 @@
         upper = strip[pl.ds(HALF, HALF)] + jnp.where(lane < N * has_u, low, 0.0)
         lower = strip[pl.ds(N, HALF)] + jnp.where(lane < N * has_d, top, 0.0)
         return jnp.concatenate([upper, lower], axis=0)
-
-    def own_light(it):
-        half = HALF // 2
-
-        def unpacked(strip, here):
-            parts = []
-            for part in range(4):
-                block = strip[pl.ds(part * half, half), :]
-                turned = pltpu.roll(block, HALF, 1)
-                parts += [turned, block] if here else [block, turned]
-            low = jnp.where(lane < N * has_u, jnp.concatenate(parts[6:], axis=0), 0.0)
-            top = jnp.where(lane < N * has_d, jnp.concatenate(parts[:2], axis=0), 0.0)
-            upper = jnp.concatenate(parts[2:4], axis=0) + low
-            lower = jnp.concatenate(parts[4:6], axis=0) + top
-            return jnp.concatenate([upper, lower], axis=0)
-
-        from_r, from_l = unpacked(lf_r.at[it], True), unpacked(lf_l.at[it], False)
-        from_up = jnp.where(lane < N * has_u, l_dn[it], 0.0)
-        from_down = jnp.where(lane < N * has_d, l_up[it], 0.0)
-        total = l_t[it, pl.ds(HALF, N), :] + jnp.concatenate([from_up, from_down], axis=0)
-        total += jnp.where(lane_n < HALF * has_l, from_l, 0.0)
-        total += jnp.where(lane_n >= N - HALF * has_r, from_r, 0.0)
-        l_sum[it] = total
 
     def update(it, old, new):
         from_l, from_r = strip_sum(f_l.at[it]), strip_sum(f_r.at[it])
@@ -369,7 +364,7 @@
             new[c] = old[c] - OBJECT_STEP * total / weight
 
     barrier = pltpu.get_barrier_semaphore()
-    greeted = [side_dev(step) for step in SIDES] + peer_dev + z_devs
+    greeted = [side_dev(step) for step in SIDES] + peer_dev + z_devs + [partner]
     for dev in greeted:
         pl.semaphore_signal(barrier, inc=1, device_id=dev, device_id_type=MESH)
     loads = [pltpu.make_async_copy(src, dst, load_sem.at[i]) for i, (src, dst) in enumerate(
@@ -380,42 +375,35 @@
     pack(0, tile_in)
     pl.semaphore_wait(barrier, len(greeted))
 
-    for copy in fetch_copies(0, tile_in):
+    for copy in fetch_copies(0, tile_in) + offset_copies():
         copy.start()
-    for channel in range(3):
+    for channel in range(2):
         for half in range(2):
             for j in range(positions):
                 pads[channel, half, j, pl.ds(0, N), :] = jnp.zeros((N, N), F32)
                 pads[channel, half, j, pl.ds(2 * N, N), :] = jnp.zeros((N, N), F32)
-    loads[1].wait()
-    light(0)
-    for copy in light_copies(0):
-        copy.start()
-
-    loads[2].wait()
-    loads[3].wait()
+    bright_pad[...] = jnp.zeros_like(bright_pad)
+    for load in loads[1:]:
+        load.wait()
+
     tiles = [tile_in, tile1, obj_out]
     for it in range(ITERS):
         for copy in fetch_copies(it, tiles[it]):
             copy.wait_recv()
         assemble(it, tiles[it])
         extract(it)
-        send_m(it)
         if it > 0:
-            wait_p(it - 1)
+            p_pair(it - 1).wait_recv()
         waves(it)
+        gradient(it)
         send_n(it)
-        send_mz(it)
-        gradient(it)
         for copy in grad_copies(it):
             copy.start()
-        if it > 0:
-            light(it)
-            for copy in light_copies(it):
-                copy.start()
-        for copy in light_copies(it):
-            copy.wait_recv()
-        own_light(it)
+        send_mz(it)
+        if it == 0:
+            for copy in offset_copies():
+                copy.wait_recv()
+        light(it)
         send_nz(it)
         for copy in grad_copies(it):
             copy.wait_recv()
@@ -425,28 +413,32 @@
             for copy in fetch_copies(it + 1, tiles[it + 1]):
                 copy.start()
         send_p(it)
-    wait_p(ITERS - 1)
+        forward_p(it)
+    p_pair(ITERS - 1).wait_recv()
     for k in range(modes):
         for c in range(2):
             prb_out[k, c] = probe_part(ITERS, k, c)
 
+    for copy in offset_copies():
+        copy.wait_send()
     for it in range(ITERS):
-        for copies in (fetch_copies(it, tiles[it]), grad_copies(it), light_copies(it)):
-            for copy in copies:
-                copy.wait_send()
+        for copy in fetch_copies(it, tiles[it]) + grad_copies(it):
+            copy.wait_send()
+        pair(0, it, m_buf.at[it], m_pre.at[it]).wait_send()
+        n_pair(it).wait_send()
+        p_pair(it).wait_send()
         await_bytes(m_rcv.at[it], all_send.at[0, it])
         await_bytes(mz_rcv.at[it], all_send.at[1, it])
         await_bytes(n_rcv.at[it], all_send.at[2, it])
         await_bytes(nz_rcv.at[it], all_send.at[3, it])
-        await_bytes(p_buf.at[it, pl.ds(0, group - 1)], all_send.at[4, it])
+        await_bytes(p_buf.at[it, 0, pl.ds(0, blocks - 1)], all_send.at[4, it])
 
 
 def per_device(n_sy, n_sx, object_tile, probe_modes, scan_offsets, intensities):
     positions = scan_offsets.shape[2]
     modes = probe_modes.shape[0]
     depth = n_sx // Y_LO
-    group = n_sy * Y_LO
-    blocks = group // modes
+    blocks = n_sy // 2 * Y_LO
     rows = N // blocks
     offsets = scan_offsets.transpose(0, 1, 3, 2)
     measured = intensities[0, 0]
@@ -455,21 +447,22 @@
     it = ITERS
     scratch = [
         vmem(object_tile.shape), vmem(probe_modes.shape), vmem(measured.shape),
-        pltpu.VMEM(tables.shape, BF16),
+        pltpu.VMEM(tables.shape, BF16), pltpu.SMEM((len(SIDES),) + offsets.shape, jnp.int32),
         vmem((2, N, N)), vmem((it, 2, 2 * N, N)), vmem((it, 2, 2 * N, N)),
         vmem((it, N, N)), vmem((it, N, N)), vmem((it, 2 * N, N)), vmem((it, 2 * N, N)),
-        vmem((positions, 2, N, N)), vmem((positions, 2, N, N)), vmem((modes, 2, N, N)),
-        vmem((3, 2, positions, 3 * N, N)), vmem((it, 2, 2 * N, N)), vmem((2, 2 * N, N)),
+        vmem((positions, 2, N, N)), vmem((modes, 2, N, N)),
+        vmem((2, 2, positions, 3 * N, N)), vmem((4 * N, N)),
+        vmem((it, 2, 2 * N, N)), vmem((2, 2 * N, N)),
         vmem((it, 2 * N, N)), vmem((it, 2 * N, N)), vmem((it, 2, HALF, N)), vmem((it, 2, HALF, N)),
-        vmem((it, 2 * N, N)), vmem((it, 2 * N, N)),
-        vmem((it, 2 * N, N)), vmem((2 * N, N)), vmem((it, N, N)), vmem((it, N, N)),
-        vmem((it, HALF, N)), vmem((it, HALF, N)),
-        vmem((it, N, N)), vmem((it, N, N)), vmem((it, N, N)),
-        vmem((it, group, 2, rows, N)), vmem((it, group - 1, 2, rows, N)), vmem((it, 2, rows, N)),
-        vmem((it, depth - 1, 2, rows, N)),
-        vmem((it, blocks, rows, N)), vmem((it, group - 1, rows, N)), vmem((it, rows, N)),
-        vmem((it, depth - 1, rows, N)), vmem((it, group, 2, rows, N)),
+        vmem((it, 2 * N, N)), vmem((it, 2 * N, N)), vmem((it, N, N)),
+        vmem((it, 2, blocks, modes, rows, N)), vmem((it, blocks, modes, rows, N)),
+        vmem((it, blocks, modes, rows, N)), vmem((it, blocks - 1, modes, rows, N)),
+        vmem((it, modes, rows, N)), vmem((it, depth - 1, modes, rows, N)),
+        vmem((it, blocks, rows, N)), vmem((it, blocks, rows, N)), vmem((it, blocks, rows, N)),
+        vmem((it, blocks - 1, rows, N)), vmem((it, rows, N)), vmem((it, depth - 1, rows, N)),
+        vmem((it, 2, blocks, modes, rows, N)),
         pltpu.SemaphoreType.DMA((3, it, len(SIDES))), pltpu.SemaphoreType.DMA((3, it, len(SIDES))),
+        pltpu.SemaphoreType.DMA((3, it)), pltpu.SemaphoreType.DMA((3, it)),
         pltpu.SemaphoreType.DMA((5, it)), pltpu.SemaphoreType.DMA((5, it)),
         pltpu.SemaphoreType.DMA((4,)),
     ]

time: 75.2 us -> 69.1 us (0.919)
  Pallas kernels: 72.1 us -> 66 us
    pallas_call x1, Pallas kernels: 72.1 us -> 66 us  [per_device(): pl.pallas_call(functools.partial(kernel, n_sy, n_sx, positions, modes), o...]
where the time goes in v3:
time: 69.1 us; the launch traced here: 68.9 us
  Pallas kernels  66 us (96%)
  local copies, waits for them, and re-layouts  2.32 us (3%)
    pallas_call x1, Pallas kernels, per_device(): pl.pallas_call(functools.partial(kernel, n_sy, n_sx, positions, modes), o...  66 us
    unnamed x4, local copies, waits for them, and re-layouts  2.32 us

profile of v3, /device:TPU:1, one launch (start us, length us, event | category | flops | bytes accessed | tf_op | source)
XLA Modules:
  0.0 68.9 jit_solution(8119786438309883987)
XLA Ops:
  0.6 66.0 %shard_map.68 = (f32[2,128,128]{2,1,0:T(8,128)}, f32[2,2,128,128]{3,2,1,0:T(8,128)}) custom-call(s32[1,1,2,4]{3,2,1,0:T(2,128)} %bitcast.3, f32[2,128,128]{2,1,0:T(8,128)} %tile_hbm.1, f32[2,2,128,128]{3,2,1,0:T(8,128)} %probe_hbm.1, f32[4,128,128]{2,1,0:T(8,128)} %bitcast.2, bf16[4,256,256]{2,1,0:T(8,128)(2,1)} %constant.2.clone.tables_hbm), custom_call_target="tpu_custom_call" | custom-call | tf_op jit(solution)/shard_map/pallas_call | solution.py:470
  66.6 0.0 copy-start
  66.6 1.6 %copy.9 = f32[2,128,128]{2,1,0:T(8,128)} copy(f32[2,128,128]{2,1,0:T(8,128)} %get-tuple-element.4) | data formatting | bytes 262144
  68.2 0.0 copy-done
  68.2 0.7 %copy.10 = f32[2,2,128,128]{3,2,1,0:T(8,128)} copy(f32[2,2,128,128]{3,2,1,0:T(8,128)S(1)} %copy-done) | data formatting | bytes 524288
Async XLA Ops:
  66.6 1.6 %copy-start = (f32[2,2,128,128]{3,2,1,0:T(8,128)S(1)}, f32[2,2,128,128]{3,2,1,0:T(8,128)}, u32[]{:S(2)}) copy-start(f32[2,2,128,128]{3,2,1,0:T(8,128)} %get-tuple-element.5) | copy-start | bytes 786436

commit v4 on v3

--- a/solution.py
+++ b/solution.py
@@ -293,31 +293,44 @@
         p_pair(it).start()
 
     def waves(it):
-        nacc[...] = jnp.zeros_like(nacc)
-
-        def position(j):
+        def right(v, t):
+            h, l = split(v)
+            return dot(h, tables[t]) + dot(l, tables[t]) + dot(h, tables[t + 1])
+
+        def right_all(vs, t):
+            if True:
+                return [right(v, t) for v in vs]
+            out = right(jnp.concatenate(vs, axis=0), t)
+            return [out[i * 2 * N:(i + 1) * 2 * N] for i in range(len(vs))]
+
+        def left(t, v):
+            h, l = split(v)
+            return dot(tables[t], h) + dot(tables[t], l) + dot(tables[t + 1], h)
+
+        def exits(j):
             o_re, o_im = obj[j, 0], obj[j, 1]
             wave = []
             for k in range(modes):
                 p_re, p_im = probe_part(it, k, 0), probe_part(it, k, 1)
                 wave.append(jnp.concatenate(
                     [p_re * o_re - p_im * o_im, p_re * o_im + p_im * o_re], axis=1))
-            x_h, x_l = split(jnp.concatenate(wave, axis=0))
-            half = dot(x_h, tables[0]) + dot(x_l, tables[0]) + dot(x_h, tables[1])
-            b_h, b_l = split(swap_blocks(half))
-            spec = dot(tables[2], b_h) + dot(tables[2], b_l) + dot(tables[3], b_h)
+            return jnp.concatenate(wave, axis=0)
+
+        def misfits(j, spec):
             power = spec[:N] * spec[:N] + spec[N:] * spec[N:]
             misfit = power[:, :N] + power[:, N:] - inten[j]
             wide = jnp.concatenate([misfit, misfit], axis=1)
-            d_h, d_l = split(jnp.concatenate([spec[:N] * wide, spec[N:] * wide], axis=0))
-            half = dot(tables[0], d_h) + dot(tables[0], d_l) + dot(tables[1], d_h)
-            e_h, e_l = split(swap_blocks(half))
-            chi = dot(e_h, tables[2]) + dot(e_l, tables[2]) + dot(e_h, tables[3])
+            return jnp.concatenate([spec[:N] * wide, spec[N:] * wide], axis=0)
+
+        def gather(j, chi, first):
+            o_re, o_im = obj[j, 0], obj[j, 1]
             g_re, g_im = None, None
             for k in range(modes):
                 c_re, c_im = chi[k * N:(k + 1) * N, :N], chi[k * N:(k + 1) * N, N:]
-                nacc[k, 0] += o_re * c_re + o_im * c_im
-                nacc[k, 1] += o_re * c_im - o_im * c_re
+                n_re = o_re * c_re + o_im * c_im
+                n_im = o_re * c_im - o_im * c_re
+                nacc[k, 0] = n_re if first else nacc[k, 0] + n_re
+                nacc[k, 1] = n_im if first else nacc[k, 1] + n_im
                 p_re, p_im = probe_part(it, k, 0), probe_part(it, k, 1)
                 a_re = p_re * c_re + p_im * c_im
                 a_im = p_re * c_im - p_im * c_re
@@ -326,10 +339,18 @@
             place(0, j, g_re)
             place(1, j, g_im)
 
-        for j in range(positions):
-            position(j)
-            if j == 0:
+        for start in range(0, positions, 4):
+            members = range(start, start + 4)
+            waves_in = [exits(j) for j in members]
+            half = [swap_blocks(v) for v in right_all(waves_in, 0)]
+            spec = [left(2, v) for v in half]
+            dev = [misfits(j, v) for j, v in zip(members, spec)]
+            if start == 0:
                 send_m(it)
+            half = [swap_blocks(left(0, v)) for v in dev]
+            chis = right_all(half, 2)
+            for j, chi in zip(members, chis):
+                gather(j, chi, j == 0)
         for k in range(modes):
             for c in range(2):
                 n_buf[it, c, :, k] = nacc[k, c].reshape(blocks, rows, N)
@@ -363,14 +384,14 @@
             total += jnp.where(lane_n >= N - HALF * has_r, right, 0.0)
             new[c] = old[c] - OBJECT_STEP * total / weight
 
+    loads = [pltpu.make_async_copy(src, dst, load_sem.at[i]) for i, (src, dst) in enumerate(
+        [(tile_hbm, tile_in), (probe_hbm, probe_in), (tables_hbm, tables), (inten_hbm, inten)])]
+    for load in loads:
+        load.start()
     barrier = pltpu.get_barrier_semaphore()
     greeted = [side_dev(step) for step in SIDES] + peer_dev + z_devs + [partner]
     for dev in greeted:
         pl.semaphore_signal(barrier, inc=1, device_id=dev, device_id_type=MESH)
-    loads = [pltpu.make_async_copy(src, dst, load_sem.at[i]) for i, (src, dst) in enumerate(
-        [(tile_hbm, tile_in), (probe_hbm, probe_in), (tables_hbm, tables), (inten_hbm, inten)])]
-    for load in loads:
-        load.start()
     loads[0].wait()
     pack(0, tile_in)
     pl.semaphore_wait(barrier, len(greeted))
@@ -397,14 +418,20 @@
         waves(it)
         gradient(it)
         send_n(it)
-        for copy in grad_copies(it):
-            copy.start()
+        if it + 1 < ITERS:
+            for copy in grad_copies(it):
+                copy.start()
         send_mz(it)
         if it == 0:
             for copy in offset_copies():
                 copy.wait_recv()
         light(it)
         send_nz(it)
+        if it + 1 == ITERS:
+            for copy in grad_copies(it):
+                copy.start()
+        if it + 1 == ITERS:
+            send_p(it)
         for copy in grad_copies(it):
             copy.wait_recv()
         update(it, tiles[it], tiles[it + 1])
@@ -412,7 +439,7 @@
             pack(it + 1, tiles[it + 1])
             for copy in fetch_copies(it + 1, tiles[it + 1]):
                 copy.start()
-        send_p(it)
+            send_p(it)
         forward_p(it)
     p_pair(ITERS - 1).wait_recv()
     for k in range(modes):
@@ -469,8 +496,7 @@
     in_vmem = pl.BlockSpec(memory_space=pltpu.VMEM)
     return pl.pallas_call(
         functools.partial(kernel, n_sy, n_sx, positions, modes),
-        out_shape=(jax.ShapeDtypeStruct(object_tile.shape, F32),
-                   jax.ShapeDtypeStruct(probe_modes.shape, F32)),
+        out_shape=(pltpu.VMEM(object_tile.shape, F32), pltpu.VMEM(probe_modes.shape, F32)),
         in_specs=[pl.BlockSpec(memory_space=pltpu.SMEM)] + [pl.BlockSpec(memory_space=pl.ANY)] * 4,
         out_specs=(in_vmem, in_vmem),
         scratch_shapes=scratch,

time: 69.1 us -> 62.3 us (0.902)
  Pallas kernels: 66 us -> 60.2 us
  local copies, waits for them, and re-layouts: 2.32 us -> 1.36 us
    pallas_call x1, Pallas kernels: 66 us -> 60.2 us  [per_device(): pl.pallas_call(functools.partial(kernel, n_sy, n_sx, positions, modes), o...]
    unnamed x4 -> x2, local copies, waits for them, and re-layouts: 2.32 us -> 1.36 us
where the time goes in v4:
time: 62.3 us; the launch traced here: 62.2 us
  Pallas kernels  60.2 us (97%)
  local copies, waits for them, and re-layouts  1.36 us (2%)
  between operations  0.64 us (1%)
    pallas_call x1, Pallas kernels, per_device(): pl.pallas_call(functools.partial(kernel, n_sy, n_sx, positions, modes), o...  60.2 us
    unnamed x2, local copies, waits for them, and re-layouts  1.36 us

profile of v4, /device:TPU:1, one launch (start us, length us, event | category | flops | bytes accessed | tf_op | source)
XLA Modules:
  0.0 62.2 jit_solution(11474197758407694767)
XLA Ops:
  0.6 60.2 %shard_map.68 = (f32[2,128,128]{2,1,0:T(8,128)S(1)}, f32[2,2,128,128]{3,2,1,0:T(8,128)S(1)}) custom-call(s32[1,1,2,4]{3,2,1,0:T(2,128)} %bitcast.3, f32[2,128,128]{2,1,0:T(8,128)} %tile_hbm.1, f32[2,2,128,128]{3,2,1,0:T(8,128)} %probe_hbm.1, f32[4,128,128]{2,1,0:T(8,128)} %bitcast.2, bf16[4,256,256]{2,1,0:T(8,128)(2,1)} %constant.2.clone.tables_hbm), custom_call_target="tpu_custom_call" | custom-call | tf_op jit(solution)/shard_map/pallas_call | solution.py:497
  60.8 0.7 %copy.9 = f32[2,128,128]{2,1,0:T(8,128)} copy(f32[2,128,128]{2,1,0:T(8,128)S(1)} %get-tuple-element.2) | data formatting | bytes 262144
  61.5 0.7 %copy.10 = f32[2,2,128,128]{3,2,1,0:T(8,128)} copy(f32[2,2,128,128]{3,2,1,0:T(8,128)S(1)} %get-tuple-element.3) | data formatting | bytes 524288

commit v5 on v4

--- a/solution.py
+++ b/solution.py
@@ -56,11 +56,11 @@
     return sorted(range(count), key=lambda d: -min(d, count - d))
 
 
-def kernel(n_sy, n_sx, positions, modes, offs, tile_hbm, probe_hbm, inten_hbm, tables_hbm,
+def kernel(n_sy, n_sx, positions, modes, offs_hbm, tile_hbm, probe_hbm, inten_hbm, tables_hbm,
            obj_out, prb_out,
-           tile_in, probe_in, inten, tables, near_offs,
+           tile_in, probe_in, inten, tables, offs, near_offs,
            tile1, can_t, can_h, pack_l, pack_r, strip_l, strip_r,
-           obj, nacc, pads, bright_pad, g_t, g_h, gp_l, gp_r, g_up, g_dn, f_l, f_r, l_sum,
+           obj, back, pads, bright_pad, g_t, g_h, gp_l, gp_r, g_up, g_dn, f_l, f_r, l_sum,
            n_buf, n_pre, n_chip, n_rcv, n_part, nz_rcv,
            m_buf, m_pre, m_chip, m_rcv, m_part, mz_rcv, p_buf,
            side_send, side_recv, pair_send, pair_recv, all_send, all_recv, load_sem):
@@ -295,17 +295,21 @@
     def waves(it):
         def right(v, t):
             h, l = split(v)
-            return dot(h, tables[t]) + dot(l, tables[t]) + dot(h, tables[t + 1])
+            count = v.shape[0]
+            both = dot(jnp.concatenate([h, l], axis=0), tables[t])
+            return both[:count] + both[count:] + dot(h, tables[t + 1])
 
         def right_all(vs, t):
-            if True:
-                return [right(v, t) for v in vs]
-            out = right(jnp.concatenate(vs, axis=0), t)
-            return [out[i * 2 * N:(i + 1) * 2 * N] for i in range(len(vs))]
+            outs = []
+            for i in range(0, len(vs), 2):
+                out = right(jnp.concatenate(vs[i:i + 2], axis=0), t)
+                outs += [out[:2 * N], out[2 * N:]]
+            return outs
 
         def left(t, v):
             h, l = split(v)
-            return dot(tables[t], h) + dot(tables[t], l) + dot(tables[t + 1], h)
+            both = dot(tables[t:t + 2].reshape(4 * N, 2 * N), h)
+            return both[:2 * N] + both[2 * N:] + dot(tables[t], l)
 
         def exits(j):
             o_re, o_im = obj[j, 0], obj[j, 1]
@@ -322,15 +326,33 @@
             wide = jnp.concatenate([misfit, misfit], axis=1)
             return jnp.concatenate([spec[:N] * wide, spec[N:] * wide], axis=0)
 
-        def gather(j, chi, first):
-            o_re, o_im = obj[j, 0], obj[j, 1]
+        members = range(positions)
+        waves_in = [exits(j) for j in members]
+        half = [swap_blocks(v) for v in right_all(waves_in, 0)]
+        spec = [left(2, v) for v in half]
+        dev = [misfits(j, v) for j, v in zip(members, spec)]
+        half = [swap_blocks(left(0, v)) for v in dev]
+        chis = right_all(half, 2)
+        for k in range(modes):
+            n_re, n_im = None, None
+            for j, chi in zip(members, chis):
+                o_re, o_im = obj[j, 0], obj[j, 1]
+                c_re, c_im = chi[k * N:(k + 1) * N, :N], chi[k * N:(k + 1) * N, N:]
+                back[j, k, 0] = c_re
+                back[j, k, 1] = c_im
+                a_re = o_re * c_re + o_im * c_im
+                a_im = o_re * c_im - o_im * c_re
+                n_re = a_re if n_re is None else n_re + a_re
+                n_im = a_im if n_im is None else n_im + a_im
+            n_buf[it, 0, :, k] = n_re.reshape(blocks, rows, N)
+            n_buf[it, 1, :, k] = n_im.reshape(blocks, rows, N)
+        n_pair(it).start()
+
+    def gradient(it):
+        for j in range(positions):
             g_re, g_im = None, None
             for k in range(modes):
-                c_re, c_im = chi[k * N:(k + 1) * N, :N], chi[k * N:(k + 1) * N, N:]
-                n_re = o_re * c_re + o_im * c_im
-                n_im = o_re * c_im - o_im * c_re
-                nacc[k, 0] = n_re if first else nacc[k, 0] + n_re
-                nacc[k, 1] = n_im if first else nacc[k, 1] + n_im
+                c_re, c_im = back[j, k, 0], back[j, k, 1]
                 p_re, p_im = probe_part(it, k, 0), probe_part(it, k, 1)
                 a_re = p_re * c_re + p_im * c_im
                 a_im = p_re * c_im - p_im * c_re
@@ -338,25 +360,6 @@
                 g_im = a_im if g_im is None else g_im + a_im
             place(0, j, g_re)
             place(1, j, g_im)
-
-        for start in range(0, positions, 4):
-            members = range(start, start + 4)
-            waves_in = [exits(j) for j in members]
-            half = [swap_blocks(v) for v in right_all(waves_in, 0)]
-            spec = [left(2, v) for v in half]
-            dev = [misfits(j, v) for j, v in zip(members, spec)]
-            if start == 0:
-                send_m(it)
-            half = [swap_blocks(left(0, v)) for v in dev]
-            chis = right_all(half, 2)
-            for j, chi in zip(members, chis):
-                gather(j, chi, j == 0)
-        for k in range(modes):
-            for c in range(2):
-                n_buf[it, c, :, k] = nacc[k, c].reshape(blocks, rows, N)
-        n_pair(it).start()
-
-    def gradient(it):
         for c in range(2):
             g_t[it, c] = placed(c, 0)
             g_h[c] = placed(c, 1)
@@ -384,16 +387,34 @@
             total += jnp.where(lane_n >= N - HALF * has_r, right, 0.0)
             new[c] = old[c] - OBJECT_STEP * total / weight
 
+    def drain():
+        for copy in offset_copies():
+            copy.wait_send()
+        for it in range(ITERS):
+            for copy in fetch_copies(it, tiles[it]) + grad_copies(it):
+                copy.wait_send()
+            pair(0, it, m_buf.at[it], m_pre.at[it]).wait_send()
+            n_pair(it).wait_send()
+            await_bytes(m_rcv.at[it], all_send.at[0, it])
+            await_bytes(mz_rcv.at[it], all_send.at[1, it])
+            await_bytes(n_rcv.at[it], all_send.at[2, it])
+            await_bytes(nz_rcv.at[it], all_send.at[3, it])
+            if it + 1 < ITERS:
+                p_pair(it).wait_send()
+                await_bytes(p_buf.at[it, 0, pl.ds(0, blocks - 1)], all_send.at[4, it])
+
+    barrier = pltpu.get_barrier_semaphore()
+    greeted = peer_dev + z_devs + [side_dev(step) for step in SIDES] + [partner]
+    for dev in greeted:
+        pl.semaphore_signal(barrier, inc=1, device_id=dev, device_id_type=MESH)
     loads = [pltpu.make_async_copy(src, dst, load_sem.at[i]) for i, (src, dst) in enumerate(
-        [(tile_hbm, tile_in), (probe_hbm, probe_in), (tables_hbm, tables), (inten_hbm, inten)])]
+        [(tile_hbm, tile_in), (offs_hbm, offs), (probe_hbm, probe_in), (tables_hbm, tables),
+         (inten_hbm, inten)])]
     for load in loads:
         load.start()
-    barrier = pltpu.get_barrier_semaphore()
-    greeted = [side_dev(step) for step in SIDES] + peer_dev + z_devs + [partner]
-    for dev in greeted:
-        pl.semaphore_signal(barrier, inc=1, device_id=dev, device_id_type=MESH)
     loads[0].wait()
     pack(0, tile_in)
+    loads[1].wait()
     pl.semaphore_wait(barrier, len(greeted))
 
     for copy in fetch_copies(0, tile_in) + offset_copies():
@@ -404,7 +425,7 @@
                 pads[channel, half, j, pl.ds(0, N), :] = jnp.zeros((N, N), F32)
                 pads[channel, half, j, pl.ds(2 * N, N), :] = jnp.zeros((N, N), F32)
     bright_pad[...] = jnp.zeros_like(bright_pad)
-    for load in loads[1:]:
+    for load in loads[2:]:
         load.wait()
 
     tiles = [tile_in, tile1, obj_out]
@@ -416,16 +437,17 @@
         if it > 0:
             p_pair(it - 1).wait_recv()
         waves(it)
+        send_m(it)
         gradient(it)
-        send_n(it)
         if it + 1 < ITERS:
             for copy in grad_copies(it):
                 copy.start()
-        send_mz(it)
+        send_n(it)
         if it == 0:
             for copy in offset_copies():
                 copy.wait_recv()
         light(it)
+        send_mz(it)
         send_nz(it)
         if it + 1 == ITERS:
             for copy in grad_copies(it):
@@ -440,25 +462,25 @@
             for copy in fetch_copies(it + 1, tiles[it + 1]):
                 copy.start()
             send_p(it)
+        if it + 1 == ITERS:
+            drain()
         forward_p(it)
     p_pair(ITERS - 1).wait_recv()
     for k in range(modes):
         for c in range(2):
             prb_out[k, c] = probe_part(ITERS, k, c)
 
-    for copy in offset_copies():
-        copy.wait_send()
-    for it in range(ITERS):
-        for copy in fetch_copies(it, tiles[it]) + grad_copies(it):
-            copy.wait_send()
-        pair(0, it, m_buf.at[it], m_pre.at[it]).wait_send()
-        n_pair(it).wait_send()
-        p_pair(it).wait_send()
-        await_bytes(m_rcv.at[it], all_send.at[0, it])
-        await_bytes(mz_rcv.at[it], all_send.at[1, it])
-        await_bytes(n_rcv.at[it], all_send.at[2, it])
-        await_bytes(nz_rcv.at[it], all_send.at[3, it])
-        await_bytes(p_buf.at[it, 0, pl.ds(0, blocks - 1)], all_send.at[4, it])
+    p_pair(ITERS - 1).wait_send()
+    await_bytes(p_buf.at[ITERS - 1, 0, pl.ds(0, blocks - 1)], all_send.at[4, ITERS - 1])
+
+
+def deliver(obj_in, prb_in, obj_out, prb_out, sem):
+    copies = [pltpu.make_async_copy(obj_in, obj_out, sem.at[0]),
+              pltpu.make_async_copy(prb_in, prb_out, sem.at[1])]
+    for copy in copies:
+        copy.start()
+    for copy in copies:
+        copy.wait()
 
 
 def per_device(n_sy, n_sx, object_tile, probe_modes, scan_offsets, intensities):
@@ -474,10 +496,11 @@
     it = ITERS
     scratch = [
         vmem(object_tile.shape), vmem(probe_modes.shape), vmem(measured.shape),
-        pltpu.VMEM(tables.shape, BF16), pltpu.SMEM((len(SIDES),) + offsets.shape, jnp.int32),
+        pltpu.VMEM(tables.shape, BF16), pltpu.SMEM(offsets.shape, jnp.int32),
+        pltpu.SMEM((len(SIDES),) + offsets.shape, jnp.int32),
         vmem((2, N, N)), vmem((it, 2, 2 * N, N)), vmem((it, 2, 2 * N, N)),
         vmem((it, N, N)), vmem((it, N, N)), vmem((it, 2 * N, N)), vmem((it, 2 * N, N)),
-        vmem((positions, 2, N, N)), vmem((modes, 2, N, N)),
+        vmem((positions, 2, N, N)), vmem((positions, modes, 2, N, N)),
         vmem((2, 2, positions, 3 * N, N)), vmem((4 * N, N)),
         vmem((it, 2, 2 * N, N)), vmem((2, 2 * N, N)),
         vmem((it, 2 * N, N)), vmem((it, 2 * N, N)), vmem((it, 2, HALF, N)), vmem((it, 2, HALF, N)),
@@ -491,17 +514,26 @@
         pltpu.SemaphoreType.DMA((3, it, len(SIDES))), pltpu.SemaphoreType.DMA((3, it, len(SIDES))),
         pltpu.SemaphoreType.DMA((3, it)), pltpu.SemaphoreType.DMA((3, it)),
         pltpu.SemaphoreType.DMA((5, it)), pltpu.SemaphoreType.DMA((5, it)),
-        pltpu.SemaphoreType.DMA((4,)),
+        pltpu.SemaphoreType.DMA((5,)),
     ]
     in_vmem = pl.BlockSpec(memory_space=pltpu.VMEM)
-    return pl.pallas_call(
+    results = pl.pallas_call(
         functools.partial(kernel, n_sy, n_sx, positions, modes),
         out_shape=(pltpu.VMEM(object_tile.shape, F32), pltpu.VMEM(probe_modes.shape, F32)),
-        in_specs=[pl.BlockSpec(memory_space=pltpu.SMEM)] + [pl.BlockSpec(memory_space=pl.ANY)] * 4,
+        in_specs=[pl.BlockSpec(memory_space=pl.ANY)] * 5,
         out_specs=(in_vmem, in_vmem),
         scratch_shapes=scratch,
         compiler_params=pltpu.CompilerParams(collective_id=0, has_side_effects=True),
     )(offsets, object_tile, probe_modes, measured, tables)
+    results = [pltpu.with_memory_space_constraint(r, pltpu.VMEM) for r in results]
+    return pl.pallas_call(
+        deliver,
+        out_shape=(jax.ShapeDtypeStruct(object_tile.shape, F32),
+                   jax.ShapeDtypeStruct(probe_modes.shape, F32)),
+        in_specs=[in_vmem, in_vmem],
+        out_specs=(pl.BlockSpec(memory_space=pl.ANY), pl.BlockSpec(memory_space=pl.ANY)),
+        scratch_shapes=[pltpu.SemaphoreType.DMA((2,))],
+    )(*results)
 
 
 def solution(mesh):

time: 62.3 us -> 60.4 us (0.970)
  local copies, waits for them, and re-layouts: 1.36 us -> 0 us
    unnamed x2 -> x0, local copies, waits for them, and re-layouts: 1.36 us -> none
    pallas_call x1, Pallas kernels: 60.2 us -> 58.9 us  [per_device(): pl.pallas_call(functools.partial(kernel, n_sy, n_sx, positions, modes), o...]
    pallas_call x0 -> x1, Pallas kernels: none -> 0.77 us  [per_device(): pl.pallas_call(deliver, out_shape=(jax.ShapeDtypeStruct(object_tile.shape...]
where the time goes in v5:
time: 60.4 us; the launch traced here: 60.3 us
  Pallas kernels  59.6 us (99%)
  between operations  0.64 us (1%)
    pallas_call x1, Pallas kernels, per_device(): pl.pallas_call(functools.partial(kernel, n_sy, n_sx, positions, modes), o...  58.9 us

profile of v5, /device:TPU:1, one launch (start us, length us, event | category | flops | bytes accessed | tf_op | source)
XLA Modules:
  0.0 60.3 jit_solution(11231512029221015216)
XLA Ops:
  0.6 58.9 %shard_map.68 = (f32[2,128,128]{2,1,0:T(8,128)S(1)}, f32[2,2,128,128]{3,2,1,0:T(8,128)S(1)}) custom-call(s32[1,1,2,4]{3,2,1,0:T(2,128)} %bitcast.3, f32[2,128,128]{2,1,0:T(8,128)} %tile_hbm.1, f32[2,2,128,128]{3,2,1,0:T(8,128)} %probe_hbm.1, f32[4,128,128]{2,1,0:T(8,128)} %bitcast.2, bf16[4,256,256]{2,1,0:T(8,128)(2,1)} %constant.2.clone.tables_hbm), custom_call_target="tpu_custom_call" | custom-call | tf_op jit(solution)/shard_map/pallas_call | solution.py:520
  59.5 0.8 %shard_map.69 = (f32[2,128,128]{2,1,0:T(8,128)}, f32[2,2,128,128]{3,2,1,0:T(8,128)}) custom-call(f32[2,128,128]{2,1,0:T(8,128)S(1)} %get-tuple-element.4.obj_in, f32[2,2,128,128]{3,2,1,0:T(8,128)S(1)} %get-tuple-element.5.prb_in), custom_call_target="tpu_custom_call" | custom-call | tf_op jit(solution)/shard_map/pallas_call | solution.py:529

commit v6 on v5

--- a/solution.py
+++ b/solution.py
@@ -63,7 +63,7 @@
            obj, back, pads, bright_pad, g_t, g_h, gp_l, gp_r, g_up, g_dn, f_l, f_r, l_sum,
            n_buf, n_pre, n_chip, n_rcv, n_part, nz_rcv,
            m_buf, m_pre, m_chip, m_rcv, m_part, mz_rcv, p_buf,
-           side_send, side_recv, pair_send, pair_recv, all_send, all_recv, load_sem):
+           side_send, side_recv, pair_send, pair_recv, all_send, all_recv, probe_recv, load_sem):
     sy = lax.axis_index("sy")
     sx = lax.axis_index("sx")
     depth = n_sx // Y_LO
@@ -86,6 +86,7 @@
     peers.sort(key=lambda p: -(min(p[0], n_x - p[0]) + min(p[1], n_y - p[1])))
     peer_index = [x_at[dx] * n_y + y_at[dy] for dx, dy in peers]
     peer_dev = [(x_at[dx] * (cores * n_yh) + y_row[dy], y_col[dy]) for dx, dy in peers]
+    from_index = [x_at[-dx] * n_y + y_at[-dy] for dx, dy in peers]
     z_devs = [(sy, y_lo * depth + lax.rem(z + d, depth)) for d in far_first(depth) if d]
     partner = (sy + 1 - 2 * core, sx)
 
@@ -243,8 +244,11 @@
     def n_pair(it):
         return pair(1, it, n_buf.at[it, 1 - core], n_pre.at[it])
 
-    def p_pair(it):
-        return pair(2, it, p_buf.at[it, core], p_buf.at[it, core])
+    def forward(it, at):
+        pair(2, it, p_buf.at[it, core, at], p_buf.at[it, core, at]).start()
+
+    def wait_p(it):
+        await_bytes(p_buf.at[it, 0], pair_recv.at[2, it])
 
     def spread(what, it, source, target):
         for slot, (other, dev) in enumerate(zip(peer_index, peer_dev)):
@@ -286,11 +290,15 @@
             else:
                 old = p_buf[it - 1, core, me, k]
             p_buf[it, core, me, k] = old - PROBE_STEP * numerator[k] / weight
-        spread(4, it, lambda other: p_buf.at[it, core, me], lambda s: p_buf.at[it, core, me])
+        mine = p_buf.at[it, core, me]
+        for slot, dev in enumerate(peer_dev):
+            remote(mine, mine, all_send.at[4, it], probe_recv.at[it, slot], dev).start()
+        forward(it, me)
 
     def forward_p(it):
-        await_bytes(p_buf.at[it, 0, pl.ds(0, blocks - 1)], all_recv.at[4, it])
-        p_pair(it).start()
+        for slot in reversed(range(blocks - 1)):
+            await_bytes(p_buf.at[it, core, from_index[slot]], probe_recv.at[it, slot])
+            forward(it, from_index[slot])
 
     def waves(it):
         def right(v, t):
@@ -400,11 +408,12 @@
             await_bytes(n_rcv.at[it], all_send.at[2, it])
             await_bytes(nz_rcv.at[it], all_send.at[3, it])
             if it + 1 < ITERS:
-                p_pair(it).wait_send()
+                await_bytes(p_buf.at[it, 0], pair_send.at[2, it])
                 await_bytes(p_buf.at[it, 0, pl.ds(0, blocks - 1)], all_send.at[4, it])
 
     barrier = pltpu.get_barrier_semaphore()
-    greeted = peer_dev + z_devs + [side_dev(step) for step in SIDES] + [partner]
+    greeted = [side_dev(step) for step in SIDES[:4]] + peer_dev + z_devs
+    greeted += [side_dev(step) for step in SIDES[4:]] + [partner]
     for dev in greeted:
         pl.semaphore_signal(barrier, inc=1, device_id=dev, device_id_type=MESH)
     loads = [pltpu.make_async_copy(src, dst, load_sem.at[i]) for i, (src, dst) in enumerate(
@@ -435,7 +444,7 @@
         assemble(it, tiles[it])
         extract(it)
         if it > 0:
-            p_pair(it - 1).wait_recv()
+            wait_p(it - 1)
         waves(it)
         send_m(it)
         gradient(it)
@@ -465,12 +474,12 @@
         if it + 1 == ITERS:
             drain()
         forward_p(it)
-    p_pair(ITERS - 1).wait_recv()
+    wait_p(ITERS - 1)
     for k in range(modes):
         for c in range(2):
             prb_out[k, c] = probe_part(ITERS, k, c)
 
-    p_pair(ITERS - 1).wait_send()
+    await_bytes(p_buf.at[ITERS - 1, 0], pair_send.at[2, ITERS - 1])
     await_bytes(p_buf.at[ITERS - 1, 0, pl.ds(0, blocks - 1)], all_send.at[4, ITERS - 1])
 
 
@@ -513,7 +522,8 @@
         vmem((it, 2, blocks, modes, rows, N)),
         pltpu.SemaphoreType.DMA((3, it, len(SIDES))), pltpu.SemaphoreType.DMA((3, it, len(SIDES))),
         pltpu.SemaphoreType.DMA((3, it)), pltpu.SemaphoreType.DMA((3, it)),
-        pltpu.SemaphoreType.DMA((5, it)), pltpu.SemaphoreType.DMA((5, it)),
+        pltpu.SemaphoreType.DMA((5, it)), pltpu.SemaphoreType.DMA((4, it)),
+        pltpu.SemaphoreType.DMA((it, blocks - 1)),
         pltpu.SemaphoreType.DMA((5,)),
     ]
     in_vmem = pl.BlockSpec(memory_space=pltpu.VMEM)

time: 60.4 us -> 60.3 us (level)
  no operation moved by 1% of the time
where the time goes in v6:
time: 60.3 us; the launch traced here: 60.2 us
  Pallas kernels  59.6 us (99%)
  between operations  0.64 us (1%)
    pallas_call x1, Pallas kernels, per_device(): pl.pallas_call(functools.partial(kernel, n_sy, n_sx, positions, modes), o...  58.8 us

profile of v6, /device:TPU:1, one launch (start us, length us, event | category | flops | bytes accessed | tf_op | source)
XLA Modules:
  0.0 60.2 jit_solution(16683928864007778633)
XLA Ops:
  0.6 58.8 %shard_map.68 = (f32[2,128,128]{2,1,0:T(8,128)S(1)}, f32[2,2,128,128]{3,2,1,0:T(8,128)S(1)}) custom-call(s32[1,1,2,4]{3,2,1,0:T(2,128)} %bitcast.3, f32[2,128,128]{2,1,0:T(8,128)} %tile_hbm.1, f32[2,2,128,128]{3,2,1,0:T(8,128)} %probe_hbm.1, f32[4,128,128]{2,1,0:T(8,128)} %bitcast.2, bf16[4,256,256]{2,1,0:T(8,128)(2,1)} %constant.2.clone.tables_hbm), custom_call_target="tpu_custom_call" | custom-call | tf_op jit(solution)/shard_map/pallas_call | solution.py:530
  59.5 0.8 %shard_map.69 = (f32[2,128,128]{2,1,0:T(8,128)}, f32[2,2,128,128]{3,2,1,0:T(8,128)}) custom-call(f32[2,128,128]{2,1,0:T(8,128)S(1)} %get-tuple-element.4.obj_in, f32[2,2,128,128]{3,2,1,0:T(8,128)S(1)} %get-tuple-element.5.prb_in), custom_call_target="tpu_custom_call" | custom-call | tf_op jit(solution)/shard_map/pallas_call | solution.py:539

commit v7 on v6

--- a/solution.py
+++ b/solution.py
@@ -308,11 +308,7 @@
             return both[:count] + both[count:] + dot(h, tables[t + 1])
 
         def right_all(vs, t):
-            outs = []
-            for i in range(0, len(vs), 2):
-                out = right(jnp.concatenate(vs[i:i + 2], axis=0), t)
-                outs += [out[:2 * N], out[2 * N:]]
-            return outs
+            return [right(v, t) for v in vs]
 
         def left(t, v):
             h, l = split(v)

time: 60.3 us -> 60.1 us (level)
  no operation moved by 1% of the time
where the time goes in v7:
time: 60.1 us; the launch traced here: 60 us
  Pallas kernels  59.4 us (99%)
  between operations  0.64 us (1%)
    pallas_call x1, Pallas kernels, per_device(): pl.pallas_call(functools.partial(kernel, n_sy, n_sx, positions, modes), o...  58.6 us

profile of v7, /device:TPU:1, one launch (start us, length us, event | category | flops | bytes accessed | tf_op | source)
XLA Modules:
  0.0 60.0 jit_solution(14267780015580133651)
XLA Ops:
  0.6 58.6 %shard_map.68 = (f32[2,128,128]{2,1,0:T(8,128)S(1)}, f32[2,2,128,128]{3,2,1,0:T(8,128)S(1)}) custom-call(s32[1,1,2,4]{3,2,1,0:T(2,128)} %bitcast.3, f32[2,128,128]{2,1,0:T(8,128)} %tile_hbm.1, f32[2,2,128,128]{3,2,1,0:T(8,128)} %probe_hbm.1, f32[4,128,128]{2,1,0:T(8,128)} %bitcast.2, bf16[4,256,256]{2,1,0:T(8,128)(2,1)} %constant.2.clone.tables_hbm), custom_call_target="tpu_custom_call" | custom-call | tf_op jit(solution)/shard_map/pallas_call | solution.py:526
  59.3 0.8 %shard_map.69 = (f32[2,128,128]{2,1,0:T(8,128)}, f32[2,2,128,128]{3,2,1,0:T(8,128)}) custom-call(f32[2,128,128]{2,1,0:T(8,128)S(1)} %get-tuple-element.4.obj_in, f32[2,2,128,128]{3,2,1,0:T(8,128)S(1)} %get-tuple-element.5.prb_in), custom_call_target="tpu_custom_call" | custom-call | tf_op jit(solution)/shard_map/pallas_call | solution.py:535

commit v8 on v6

--- a/solution.py
+++ b/solution.py
@@ -75,8 +75,15 @@
     y_lo = lax.div(sx, depth)
     y = lax.rem(lax.div(sy, cores), n_yh) * Y_LO + y_lo
     z = lax.rem(sx, depth)
-    x_at = [lax.rem(x + d, n_x) for d in range(n_x)]
-    y_at = [lax.rem(y + d, n_y) for d in range(n_y)]
+    def up(value, count):
+        return jnp.where(value >= count, value - count, value)
+
+    def wrap(value, count, step):
+        return up(value + step, count) if step >= 0 else jnp.where(
+            value + step < 0, value + step + count, value + step)
+
+    x_at = [wrap(x, n_x, d) for d in range(n_x)]
+    y_at = [wrap(y, n_y, d) for d in range(n_y)]
     y_row = [lax.div(v, Y_LO) * cores + core for v in y_at]
     y_col = [lax.rem(v, Y_LO) * depth + z for v in y_at]
     blocks = n_x * n_y
@@ -87,12 +94,14 @@
     peer_index = [x_at[dx] * n_y + y_at[dy] for dx, dy in peers]
     peer_dev = [(x_at[dx] * (cores * n_yh) + y_row[dy], y_col[dy]) for dx, dy in peers]
     from_index = [x_at[-dx] * n_y + y_at[-dy] for dx, dy in peers]
-    z_devs = [(sy, y_lo * depth + lax.rem(z + d, depth)) for d in far_first(depth) if d]
+    z_devs = [(sy, y_lo * depth + wrap(z, depth, d)) for d in far_first(depth) if d]
     partner = (sy + 1 - 2 * core, sx)
 
+    row_at = {d: wrap(sy, n_sy, d) for d in (-1, 0, 1)}
+    col_at = {d: wrap(sx, n_sx, d) for d in (-1, 0, 1)}
+
     def side_dev(step):
-        dy, dx = step
-        return (lax.rem(sy + (n_sy + dy), n_sy), lax.rem(sx + (n_sx + dx), n_sx))
+        return (row_at[step[0]], col_at[step[1]])
 
     lane = lax.broadcasted_iota(jnp.int32, (HALF, N), 1)
     lane_n = lax.broadcasted_iota(jnp.int32, (N, N), 1)
@@ -413,7 +422,7 @@
 
     barrier = pltpu.get_barrier_semaphore()
     greeted = [side_dev(step) for step in SIDES[:4]] + peer_dev + z_devs
-    greeted += [side_dev(step) for step in SIDES[4:]] + [partner]
+    greeted += [side_dev(step) for step in SIDES[4:]]
     for dev in greeted:
         pl.semaphore_signal(barrier, inc=1, device_id=dev, device_id_type=MESH)
     loads = [pltpu.make_async_copy(src, dst, load_sem.at[i]) for i, (src, dst) in enumerate(

time: 60.3 us -> 60.3 us (level)
  no operation moved by 1% of the time
where the time goes in v8:
time: 60.3 us; the launch traced here: 60.2 us
  Pallas kernels  59.6 us (99%)
  between operations  0.64 us (1%)
    pallas_call x1, Pallas kernels, per_device(): pl.pallas_call(functools.partial(kernel, n_sy, n_sx, positions, modes), o...  58.8 us

profile of v8, /device:TPU:1, one launch (start us, length us, event | category | flops | bytes accessed | tf_op | source)
XLA Modules:
  0.0 60.2 jit_solution(14067810165926268784)
XLA Ops:
  0.6 58.8 %shard_map.68 = (f32[2,128,128]{2,1,0:T(8,128)S(1)}, f32[2,2,128,128]{3,2,1,0:T(8,128)S(1)}) custom-call(s32[1,1,2,4]{3,2,1,0:T(2,128)} %bitcast.3, f32[2,128,128]{2,1,0:T(8,128)} %tile_hbm.1, f32[2,2,128,128]{3,2,1,0:T(8,128)} %probe_hbm.1, f32[4,128,128]{2,1,0:T(8,128)} %bitcast.2, bf16[4,256,256]{2,1,0:T(8,128)(2,1)} %constant.2.clone.tables_hbm), custom_call_target="tpu_custom_call" | custom-call | tf_op jit(solution)/shard_map/pallas_call | solution.py:539
  59.4 0.8 %shard_map.69 = (f32[2,128,128]{2,1,0:T(8,128)}, f32[2,2,128,128]{3,2,1,0:T(8,128)}) custom-call(f32[2,128,128]{2,1,0:T(8,128)S(1)} %get-tuple-element.4.obj_in, f32[2,2,128,128]{3,2,1,0:T(8,128)S(1)} %get-tuple-element.5.prb_in), custom_call_target="tpu_custom_call" | custom-call | tf_op jit(solution)/shard_map/pallas_call | solution.py:548

commit v9 on v8

--- a/solution.py
+++ b/solution.py
@@ -317,11 +317,7 @@
             return both[:count] + both[count:] + dot(h, tables[t + 1])
 
         def right_all(vs, t):
-            outs = []
-            for i in range(0, len(vs), 2):
-                out = right(jnp.concatenate(vs[i:i + 2], axis=0), t)
-                outs += [out[:2 * N], out[2 * N:]]
-            return outs
+            return [right(v, t) for v in vs]
 
         def left(t, v):
             h, l = split(v)

time: 60.3 us -> 60.1 us (level)
  no operation moved by 1% of the time
where the time goes in v9:
time: 60.1 us; the launch traced here: 60 us
  Pallas kernels  59.4 us (99%)
  between operations  0.64 us (1%)
    pallas_call x1, Pallas kernels, per_device(): pl.pallas_call(functools.partial(kernel, n_sy, n_sx, positions, modes), o...  58.6 us

profile of v9, /device:TPU:1, one launch (start us, length us, event | category | flops | bytes accessed | tf_op | source)
XLA Modules:
  0.0 60.0 jit_solution(13222943084444698632)
XLA Ops:
  0.6 58.6 %shard_map.68 = (f32[2,128,128]{2,1,0:T(8,128)S(1)}, f32[2,2,128,128]{3,2,1,0:T(8,128)S(1)}) custom-call(s32[1,1,2,4]{3,2,1,0:T(2,128)} %bitcast.3, f32[2,128,128]{2,1,0:T(8,128)} %tile_hbm.1, f32[2,2,128,128]{3,2,1,0:T(8,128)} %probe_hbm.1, f32[4,128,128]{2,1,0:T(8,128)} %bitcast.2, bf16[4,256,256]{2,1,0:T(8,128)(2,1)} %constant.2.clone.tables_hbm), custom_call_target="tpu_custom_call" | custom-call | tf_op jit(solution)/shard_map/pallas_call | solution.py:535
  59.3 0.8 %shard_map.69 = (f32[2,128,128]{2,1,0:T(8,128)}, f32[2,2,128,128]{3,2,1,0:T(8,128)}) custom-call(f32[2,128,128]{2,1,0:T(8,128)S(1)} %get-tuple-element.4.obj_in, f32[2,2,128,128]{3,2,1,0:T(8,128)S(1)} %get-tuple-element.5.prb_in), custom_call_target="tpu_custom_call" | custom-call | tf_op jit(solution)/shard_map/pallas_call | solution.py:544
